TPU v7x, 32 devices: a whole 2x2x4 slice. The times are simulated.
32 devices in a mesh: gx: 4 (over x, core), gy: 2 (over y), gz: 4 (over z).
Axes of the slice: x: 2, y: 2, z: 4, core: 2. Of those that a mesh axis runs over, the one named last changes fastest.
Arguments:
- features: bfloat16 [4, 2, 4, 16, 3200], P('gx', 'gy', 'gz'), may hold values from -6 to 6
- box_atoms: int32 [4, 2, 4], P('gx', 'gy', 'gz'), may hold values from 5 to 16, as said below
- edge_count: int32 [4, 2, 4], P('gx', 'gy', 'gz'), may hold values from 85 to 256, as said below
- edge_tower: int32 [4, 2, 4, 256], P('gx', 'gy', 'gz'), may hold values from 0 to 47, as said below
- edge_plate: int32 [4, 2, 4, 256], P('gx', 'gy', 'gz'), may hold values from 0 to 143, as said below
- wigner: float32 [4, 2, 4, 115, 256], P('gx', 'gy', 'gz'), may hold values from -1 to 1, as said below
- radial: bfloat16 [4, 2, 4, 256, 128], P('gx', 'gy', 'gz'), may hold values from 0.049804688 to 0.5
- so2_zero: bfloat16 [640, 640], replicated, may hold values from -0.25 to 0.25
- so2_one: bfloat16 [2, 512, 512], replicated, may hold values from -0.1875 to 0.1875
- so2_two: bfloat16 [2, 384, 384], replicated, may hold values from -0.21875 to 0.21875
Outputs:
- updated: bfloat16 [4, 2, 4, 16, 3200], P('gx', 'gy', 'gz')
Inputs may be any that keep to these rules, and one draw needn't show every extreme that they name: `box_atoms`: the fullest box holds exactly 16 atoms in every draw; counts span a factor of three. `edge_count`: some device holds exactly 256 live edges in every draw. `edge_tower`: every entry d * 16 + a names an atom a present in tower box d, in live and padded slots alike. `edge_plate`: every entry p * 16 + a names an atom a present in plate box p, in live and padded slots alike. `wigner`: for each edge and degree, the rows are rows of an orthogonal matrix.
All inputs are finite; a program needn't handle non-finite values.
Results may differ from a plain program's by a relative error of at most 0.007.
Values may be sent and summed in bfloat16 or wider, within the bound.
No kernel may reach another device: no remote copies, remote signals or barrier semaphores. Data moves between devices by JAX's collectives and lax.ppermute only.
A program may use at most 64 MiB of HBM per device.

v0:
```python
import functools

import jax
import jax.numpy as jnp
from jax import lax
from jax.experimental import pallas as pl
from jax.experimental.pallas import tpu as pltpu
from jax.sharding import PartitionSpec as P


DEGREE = 4
ORDER = 2
COEFS = (DEGREE + 1) ** 2
LAST_LAST = (((1,), (1,)), ((), ()))


def steps_of(axis):
    return (0, 1, -1)[: min(lax.axis_size(axis), 3)]


def place_of(axis):
    return [(0, 0, 0), (1, 0, 1), (2, 0, 1)][min(lax.axis_size(axis), 3) - 1]


def hand_on(block, axis, distance):
    count = lax.axis_size(axis)
    return lax.ppermute(block, axis, [(i, (i + distance) % count) for i in range(count)])


def entries():
    found = []
    for degree in range(DEGREE + 1):
        within = min(degree, ORDER)
        for azimuth in range(-within, within + 1):
            found += [(degree, azimuth, column) for column in range(2 * degree + 1)]
    return found


def offset_of(degree, azimuth):
    return entries().index((degree, azimuth, 0))


def whole(shape):
    return pl.BlockSpec(shape, lambda: (0,) * len(shape), memory_space=pltpu.VMEM)


def prepare_kernel(
    tower_classes, plate_classes, opened, count, present, tower_ref, plate_ref, features, wigner, radial, zero, one, two,
    tower_pick, plate_pick, mask, own, spread, gate, zero_t, one_t, two_t,
    count_here, present_here, wigner_here, radial_here, zero_here, one_here, two_here, arrived,
):
    loads = [
        pltpu.make_async_copy(there, here, arrived.at[place])
        for place, (there, here) in enumerate(
            (
                (count, count_here),
                (present, present_here),
                (features, own),
                (wigner, wigner_here),
                (radial, radial_here),
                (zero, zero_here),
                (one, one_here),
                (two, two_here),
            )
        )
    ]
    for load in loads:
        load.start()
    edges = radial.shape[0]
    loads[0].wait()
    loads[1].wait()
    live = lax.broadcasted_iota(jnp.int32, (1, edges), 1) < count_here[...]
    row = lax.broadcasted_iota(jnp.int32, mask.shape, 0)
    mask[...] = jnp.where(row < present_here[...], 1.0, 0.0)
    for index_ref, classes, pick in (
        (tower_ref, tower_classes, tower_pick),
        (plate_ref, plate_classes, plate_pick),
    ):
        index = jnp.where(live, index_ref[...], -1)
        atoms = pick.shape[0] // len(classes)
        atom = lax.broadcasted_iota(jnp.int32, (atoms, edges), 0)
        for place, slots in enumerate(classes):
            hit = functools.reduce(
                jnp.logical_or, [index == atom + slot * atoms for slot in slots]
            )
            pick[place * atoms : (place + 1) * atoms, :] = jnp.where(hit, 1.0, 0.0).astype(pick.dtype)

    def copy_row(k, carry):
        spread[k] = jnp.broadcast_to(wigner_here[k], spread.shape[1:])
        return carry

    loads[2].wait()
    loads[3].wait()
    lax.fori_loop(0, spread.shape[0], copy_row, 0, unroll=5)
    loads[4].wait()
    gate[...] = radial_here[...].astype(jnp.float32).T
    loads[5].wait()
    zero_t[...] = zero_here[...].T
    for load, ref, out in ((loads[6], one_here, one_t), (loads[7], two_here, two_t)):
        load.wait()
        width = ref.shape[1]
        for part in range(2):
            out[:, part * width : (part + 1) * width] = ref[part].T


GROUP = 16


def rows(at):
    return pl.ds(pl.multiple_of(at, GROUP), GROUP)


def side_kernel(pieces, shares, *refs):
    piece_refs, refs = refs[:pieces], refs[pieces:]
    from_pick, to_pick, spread, gate, zero_t, one_t, two_t, *refs = refs
    outs, refs = refs[: len(shares)], refs[len(shares) :]
    source, even, odd, low_zero, low_one, low_two, mixed, message = refs
    channels, edges = gate.shape
    lanes = 128
    for k in range(COEFS):
        at = slice(k * channels, (k + 1) * channels)
        block = jnp.concatenate([ref[:, at] for ref in piece_refs], axis=0)
        source[at, :] = block.T

    def gather(i, out):
        picked = jnp.concatenate([source[rows(k * channels + i * GROUP), :] for k in range(COEFS)], axis=0)
        out[...] = jnp.dot(picked, from_pick[...], preferred_element_type=jnp.float32)

    def forward(i, turned):
        start = i * GROUP
        for piece in range(edges // lanes):
            here_lanes = slice(piece * lanes, (piece + 1) * lanes)
            far_lanes = slice(edges + piece * lanes, edges + (piece + 1) * lanes)
            here = gate[rows(start), here_lanes]
            for degree in range(DEGREE + 1):
                within = min(degree, ORDER)
                span = 2 * degree + 1
                first_coef = degree * degree
                values = [
                    turned[(first_coef + c) * GROUP : (first_coef + c + 1) * GROUP, here_lanes]
                    for c in range(span)
                ]
                for azimuth in range(-within, within + 1):
                    k = offset_of(degree, azimuth)
                    total = None
                    for c in range(span):
                        turn = spread[k + c, :, here_lanes]
                        term = jnp.concatenate([turn, turn], axis=0) * values[c]
                        total = term if total is None else total + term
                    low = total * here
                    small = low.astype(jnp.bfloat16)
                    if azimuth == 0:
                        low_zero[rows(degree * channels + start), here_lanes] = small
                        continue
                    order = abs(azimuth)
                    ref = low_one if order == 1 else low_two
                    at = (degree - order) * channels + start
                    first, second = rows(at), rows(ref.shape[0] // 2 + at)
                    if azimuth > 0:
                        ref[first, here_lanes] = small
                        ref[second, far_lanes] = small
                    else:
                        ref[first, far_lanes] = small
                        ref[second, here_lanes] = -small

    groups = channels // GROUP
    gather(0, even)

    def pair(j, carry):
        gather(2 * j + 1, odd)
        forward(2 * j, even)
        gather(jnp.minimum(2 * j + 2, groups - 1), even)
        forward(2 * j + 1, odd)
        return carry

    lax.fori_loop(0, groups // 2, pair, 0)

    mixed[: low_zero.shape[0], :] = jnp.dot(
        zero_t[...], low_zero[...], preferred_element_type=jnp.float32
    )
    base = low_zero.shape[0]
    bases = {0: 0}
    for order, table, low in ((1, one_t, low_one), (2, two_t, low_two)):
        height = table.shape[0]
        for sign in range(2):
            mixed[base : base + height, :] = jnp.dot(
                table[...], low[:, sign * edges : (sign + 1) * edges],
                preferred_element_type=jnp.float32,
            )
            bases[order if sign == 0 else -order] = base
            base += height

    def backward(i, carry):
        start = i * GROUP
        for piece in range(edges // lanes):
            here_lanes = slice(piece * lanes, (piece + 1) * lanes)
            for degree in range(DEGREE + 1):
                within = min(degree, ORDER)
                span = 2 * degree + 1
                values = {}
                for azimuth in range(-within, within + 1):
                    at = bases[azimuth] + (degree - abs(azimuth)) * channels + start
                    values[azimuth] = mixed[rows(at), here_lanes]
                for c in range(span):
                    total = None
                    for azimuth in range(-within, within + 1):
                        turn = spread[offset_of(degree, azimuth) + c, :, here_lanes]
                        term = jnp.concatenate([turn, turn], axis=0) * values[azimuth]
                        total = term if total is None else total + term
                    at = (degree * degree + c) * channels + start
                    message[rows(at), here_lanes] = total.astype(jnp.bfloat16)
        return carry

    lax.fori_loop(0, groups, backward, 0)

    spot = to_pick[...]
    step = 5 * channels
    for at in range(0, COEFS * channels, step):
        total = lax.dot_general(
            spot, message[at : at + step, :], LAST_LAST, preferred_element_type=jnp.float32
        )
        for out, share in zip(outs, shares):
            atoms = out.shape[0] // len(share)
            for place, box in enumerate(share):
                out[place * atoms : (place + 1) * atoms, at : at + step] = total[
                    box * atoms : (box + 1) * atoms, :
                ].astype(out.dtype)


def one_side(pieces, from_pick, to_pick, prepared, shares, atoms):
    gate = prepared[1]
    channels, edges = gate.shape
    width = pieces[0].shape[1]
    operands = [*pieces, from_pick, to_pick, *prepared]
    outs = tuple(jax.ShapeDtypeStruct((len(boxes) * atoms, width), dtype) for boxes, dtype in shares)
    orders = DEGREE + 1 + sum(2 * (DEGREE + 1 - m) for m in range(1, ORDER + 1))
    work = channels * edges * 2
    flops = work * (sum((DEGREE + 1 - m) ** 2 * channels * (4 if m else 1) for m in range(ORDER + 1)))
    return pl.pallas_call(
        functools.partial(side_kernel, len(pieces), [boxes for boxes, dtype in shares]),
        out_shape=outs,
        in_specs=[whole(o.shape) for o in operands],
        out_specs=tuple(whole(o.shape) for o in outs),
        scratch_shapes=[
            pltpu.VMEM((width, from_pick.shape[0]), jnp.bfloat16),
            pltpu.VMEM((COEFS * GROUP, edges), jnp.float32),
            pltpu.VMEM((COEFS * GROUP, edges), jnp.float32),
            pltpu.VMEM(((DEGREE + 1) * channels, edges), jnp.bfloat16),
            pltpu.VMEM((2 * DEGREE * channels, 2 * edges), jnp.bfloat16),
            pltpu.VMEM((2 * (DEGREE - 1) * channels, 2 * edges), jnp.bfloat16),
            pltpu.VMEM((orders * channels, edges), jnp.float32),
            pltpu.VMEM((COEFS * channels, edges), jnp.bfloat16),
        ],
        compiler_params=pltpu.CompilerParams(vmem_limit_bytes=40 * 1024 * 1024),
        cost_estimate=pl.CostEstimate(flops=flops, bytes_accessed=8 << 20, transcendentals=0),
    )(*operands)


def opening_kernel(out):
    out[...] = jnp.zeros_like(out)


def opening():
    return pl.pallas_call(
        opening_kernel,
        out_shape=jax.ShapeDtypeStruct((8, 128), jnp.float32),
        out_specs=whole((8, 128)),
        compiler_params=pltpu.CompilerParams(vmem_limit_bytes=1024 * 1024),
        cost_estimate=pl.CostEstimate(flops=20000000000, bytes_accessed=4096, transcendentals=0),
        name="opening",
    )()


def prepare(
    edge_count, box_atoms, edge_tower, edge_plate, own, wigner, radial, zero, one, two, tower_classes, plate_classes
):
    edges, channels = radial.shape
    atoms = own.shape[0]
    shape = jax.ShapeDtypeStruct
    opened = opening()
    operands = [edge_count, box_atoms, edge_tower, edge_plate, own, wigner, radial, zero, one, two]
    outs = (
        shape((len(tower_classes) * atoms, edges), jnp.bfloat16),
        shape((len(plate_classes) * atoms, edges), jnp.bfloat16),
        shape((atoms, 128), jnp.float32),
        shape(own.shape, own.dtype),
        shape((wigner.shape[0], 8, edges), jnp.float32),
        shape((channels, edges), jnp.float32),
        shape(zero.shape, jnp.bfloat16),
        shape((one.shape[1], 2 * one.shape[1]), jnp.bfloat16),
        shape((two.shape[1], 2 * two.shape[1]), jnp.bfloat16),
    )
    there = pl.BlockSpec(memory_space=pltpu.HBM)
    return pl.pallas_call(
        functools.partial(prepare_kernel, tower_classes, plate_classes),
        out_shape=outs,
        in_specs=[whole(opened.shape)] + [there] * 2 + [whole(o.shape) for o in operands[2:4]] + [there] * 6,
        out_specs=tuple(whole(o.shape) for o in outs),
        scratch_shapes=[pltpu.VMEM(o.shape, o.dtype) for o in operands[:2] + operands[5:]]
        + [pltpu.SemaphoreType.DMA((8,))],
        compiler_params=pltpu.CompilerParams(vmem_limit_bytes=24 * 1024 * 1024),
        cost_estimate=pl.CostEstimate(flops=1 << 20, bytes_accessed=8 << 20, transcendentals=0),
        name="prepare",
    )(opened, *operands)


def body(
    features,
    box_atoms,
    edge_count,
    edge_tower,
    edge_plate,
    wigner,
    radial,
    so2_zero,
    so2_one,
    so2_two,
):
    atoms = features.shape[3]
    width = features.shape[4]
    edges = edge_tower.shape[3]
    start = features.reshape(atoms, width)
    x_steps, y_steps, z_steps = steps_of("gx"), steps_of("gy"), steps_of("gz")
    x_place, y_place, z_place = place_of("gx"), place_of("gy"), place_of("gz")
    tower_classes = [[s for s in range(3) if x_place[s] == p] for p in range(len(x_steps))]
    plate_classes = [
        [3 * e + f for e in range(3) for f in range(3) if (y_place[e], z_place[f]) == (py, pz)]
        for pz in range(len(z_steps))
        for py in range(len(y_steps))
    ]

    beside = [hand_on(start, "gy", -step) for step in y_steps[1:]]
    tower = [hand_on(start, "gx", -step) for step in x_steps[1:]]
    tower_pick, plate_pick, mask, own, *prepared = prepare(
        edge_count.reshape(1, 1),
        box_atoms.reshape(1, 1),
        edge_tower.reshape(1, edges),
        edge_plate.reshape(1, edges),
        start,
        wigner.reshape(wigner.shape[3], 1, edges),
        radial.reshape(edges, radial.shape[4]),
        so2_zero,
        so2_one,
        so2_two,
        tower_classes,
        plate_classes,
    )
    column = jnp.concatenate([own] + beside)
    columns = [hand_on(column, "gz", -step) for step in z_steps[1:]]

    across = len(y_steps)
    ends = range(1, len(z_steps))
    here = [([pz * across], jnp.float32) for pz in range(len(z_steps))]
    there = [
        share
        for py in range(1, across)
        for share in (([pz * across + py for pz in ends], jnp.bfloat16), ([py], jnp.bfloat16))
    ]
    sums = one_side([own] + tower, tower_pick, plate_pick, prepared, here + there, atoms)
    kept, leaving = sums[: len(here)], sums[len(here) :]
    kept = list(kept)
    for p, step in enumerate(y_steps[1:]):
        side = hand_on(leaving[2 * p], "gy", step)
        middle = hand_on(leaving[2 * p + 1], "gy", step)
        kept[0] = kept[0] + middle
        for pz in ends:
            kept[pz] = kept[pz] + side[(pz - 1) * atoms : pz * atoms]
    plate_total = kept[0]
    for p, step in enumerate(z_steps[1:]):
        plate_total = plate_total + hand_on(kept[p + 1].astype(jnp.bfloat16), "gz", step)

    shares = [([0], jnp.float32)] + [([p], jnp.bfloat16) for p in range(1, len(x_steps))]
    gathered, *leaving = one_side([own] + beside + columns, plate_pick, tower_pick, prepared, shares, atoms)
    for p, step in enumerate(x_steps[1:]):
        gathered = gathered + hand_on(leaving[p], "gx", step)
    updated = own.astype(jnp.float32) + (gathered + plate_total)
    return jnp.where(mask[:, :1] > 0, updated, 0.0).astype(jnp.bfloat16).reshape(features.shape)


def solution(mesh):
    boxes = P("gx", "gy", "gz")
    placed = (
        P("gx", "gy", "gz", None, None),
        boxes,
        boxes,
        P("gx", "gy", "gz", None),
        P("gx", "gy", "gz", None),
        P("gx", "gy", "gz", None, None),
        P("gx", "gy", "gz", None, None),
        P(),
        P(),
        P(),
    )

    return jax.shard_map(body, mesh=mesh, in_specs=placed, out_specs=P("gx", "gy", "gz", None, None), check_vma=False)
```

profile of v0, /device:TPU:0, one launch (start us, length us, event | category | flops | bytes accessed | tf_op | source)
XLA Modules:
  0.0 39.6 jit_solution(4948013841102747308)
XLA Ops:
  0.0 0.0 copy-start
  0.0 0.0 copy-start.1
  0.0 0.0 copy-start.2
  0.0 0.0 copy-start.3
  0.0 0.0 copy-start.4
  0.0 0.0 copy-start.5
  0.0 2.5 %collective-permute-start.5 = (bf16[16,3200]{1,0:T(8,128)(2,1)}, bf16[16,3200]{1,0:T(8,128)(2,1)S(1)}, u32[]{:S(2)}, u32[]{:S(2)}) collective-permute-start(bf16[16,3200]{1,0:T(8,128)(2,1)} %bitcast.12), channel_id=1, source_target_pairs={{0,24},{8,0},{16,8},{24,16},{1,25},{9,1},{17,9},{25,17},{2,26},{10... | collective-permute-start | bytes 307208 | tf_op jit(solution)/shard_map/ppermute | solution.py:27
  2.5 0.0 collective-permute-start.6
  2.5 1.5 %collective-permute-start = (bf16[16,3200]{1,0:T(8,128)(2,1)}, bf16[16,3200]{1,0:T(8,128)(2,1)S(1)}, u32[]{:S(2)}, u32[]{:S(2)}) collective-permute-start(bf16[16,3200]{1,0:T(8,128)(2,1)} %bitcast.14), channel_id=1, source_target_pairs={{0,4},{4,0},{1,5},{5,1},{2,6},{6,2},{3,7},{7,3},{8,12},{12,8},{9,1... | collective-permute-start | bytes 307208 | tf_op jit(solution)/shard_map/ppermute | solution.py:27
  4.0 0.0 copy-start.7
  5.3 0.0 copy-start.6
  5.3 0.0 copy-done
  5.4 0.0 copy-done.1
  5.4 0.0 copy-done.2
  5.4 0.0 copy-done.3
  5.4 0.0 copy-done.4
  5.4 0.0 copy-done.5
  5.4 0.0 copy-done.7
  5.4 0.6 %copy-done.6 = s32[1,1,1,256]{3,2,1,0:T(1,128)S(1)} copy-done((s32[1,1,1,256]{3,2,1,0:T(1,128)S(1)}, s32[1,1,1,256]{3,2,1,0:T(1,128)}, u32[]{:S(2)}) %copy-start.6) | copy-done | bytes 1048
  6.0 1.9 %prepare.1 = (bf16[48,256]{1,0:T(8,128)(2,1)S(1)}, bf16[96,256]{1,0:T(8,128)(2,1)S(1)}, f32[16,128]{1,0:T(8,128)S(1)}, bf16[16,3200]{1,0:T(8,128)(2,1)S(1)}, f32...) custom-call(f32[8,128]{1,0:T(8,128)S(1)} %opening.1.opened, ...), custom_call_target="tpu_custom_call" | custom-call | flops 1048576 | bytes 8388608 | tf_op jit(solution)/shard_map/prepare/pallas_call | solution.py:294
  8.0 0.0 collective-permute-done.5.refs_1_
  8.0 0.0 collective-permute-done.6.refs_2_
  8.0 5.3 %shard_map.101 = (f32[16,3200]{1,0:T(8,128)S(1)}, f32[16,3200]{1,0:T(8,128)S(1)}, f32[16,3200]{1,0:T(8,128)S(1)}, bf16[32,3200]{1,0:T(8,128)(2,1)S(1)}, bf16[16,3200]{1,0:T(8,128)(2,1)S(1)}) custom-call(bf16[16,3200]{1,0:T(8,128)(2,1)S(1)} %get-tuple-element.23.refs_0_, bf16[16,3200]{1,0:T(8,128)(2,1)S(1)} %collective-permute-done.5.refs_1_, ...), custom_call_target="tpu_custom_call" | custom-call | flops 1048576000 | bytes 8388608 | tf_op jit(solution)/shard_map/pallas_call | solution.py:239
  13.3 0.6 %collective-permute-start.8 = (bf16[32,3200]{1,0:T(8,128)(2,1)S(1)}, bf16[32,3200]{1,0:T(8,128)(2,1)S(1)}, u32[]{:S(2)}, u32[]{:S(2)}) collective-permute-start(bf16[32,3200]{1,0:T(8,128)(2,1)S(1)} %get-tuple-element.37), channel_id=1, source_target_pairs={{0,4},{4,0},{1,5},{5,1},{2,6},{6,2},{3,7},{7,3},{8,12},{12,8},{9,1... | collective-permute-start | bytes 614408 | tf_op jit(solution)/shard_map/ppermute | solution.py:27
  13.9 0.0 collective-permute-done.refs_1_
  13.9 3.7 %collective-permute-start.1 = (bf16[32,3200]{1,0:T(8,128)(2,1)S(1)}, bf16[32,3200]{1,0:T(8,128)(2,1)S(1)}, u32[]{:S(2)}, u32[]{:S(2)}) collective-permute-start(bf16[32,3200]{1,0:T(8,128)(2,1)S(1)} %constant_dynamic-update-slice_fusion), channel_id=1, source_target_pairs={{0,3},{1,0},{2,1},{3,2},{4,7},{5,4},{6,5},{7,6},{8,11},{9,8},{10,9... | collective-permute-start | bytes 614408 | tf_op jit(solution)/shard_map/ppermute | solution.py:27
  17.5 0.0 collective-permute-start.2
  17.5 1.5 %collective-permute-start.7 = (bf16[16,3200]{1,0:T(8,128)(2,1)S(1)}, bf16[16,3200]{1,0:T(8,128)(2,1)S(1)}, u32[]{:S(2)}, u32[]{:S(2)}) collective-permute-start(bf16[16,3200]{1,0:T(8,128)(2,1)S(1)} %get-tuple-element.35), channel_id=1, source_target_pairs={{0,4},{4,0},{1,5},{5,1},{2,6},{6,2},{3,7},{7,3},{8,12},{12,8},{9,1... | collective-permute-start | bytes 307208 | tf_op jit(solution)/shard_map/ppermute | solution.py:27
  19.0 2.2 %collective-permute-done.8 = bf16[32,3200]{1,0:T(8,128)(2,1)S(1)} collective-permute-done((bf16[32,3200]{1,0:T(8,128)(2,1)S(1)}, bf16[32,3200]{1,0:T(8,128)(2,1)S(1)}, u32[]{:S(2)}, u32[]{:S(2)}) %collective-permute-start.8) | collective-permute-done | bytes 204832 | tf_op jit(solution)/shard_map/ppermute | solution.py:27
  21.3 0.1 add_convert_fusion.1
  21.3 3.7 %collective-permute-start.10 = (bf16[16,3200]{1,0:T(8,128)(2,1)S(1)}, bf16[16,3200]{1,0:T(8,128)(2,1)S(1)}, u32[]{:S(2)}, u32[]{:S(2)}) collective-permute-start(bf16[16,3200]{1,0:T(8,128)(2,1)S(1)} %get-tuple-element.40), channel_id=1, source_target_pairs={{0,3},{1,0},{2,1},{3,2},{4,7},{5,4},{6,5},{7,6},{8,11},{9,8},{10,9... | collective-permute-start | bytes 307208 | tf_op jit(solution)/shard_map/ppermute | solution.py:27
  25.0 0.0 collective-permute-start.9
  25.0 0.0 collective-permute-done.1.refs_2_
  25.0 3.4 %collective-permute-done.2.refs_3_ = bf16[32,3200]{1,0:T(8,128)(2,1)S(1)} collective-permute-done((bf16[32,3200]{1,0:T(8,128)(2,1)S(1)}, bf16[32,3200]{1,0:T(8,128)(2,1)S(1)}, u32[]{:S(2)}, u32[]{:S(2)}) %collective-permute-start.2) | collective-permute-done | bytes 204832 | tf_op jit(solution)/shard_map/ppermute | solution.py:27
  28.3 5.3 %shard_map.100 = (f32[16,3200]{1,0:T(8,128)S(1)}, bf16[16,3200]{1,0:T(8,128)(2,1)S(1)}, bf16[16,3200]{1,0:T(8,128)(2,1)S(1)}) custom-call(bf16[16,3200]{1,0:T(8,128)(2,1)S(1)} %get-tuple-element.23.refs_0_, bf16[16,3200]{1,0:T(8,128)(2,1)S(1)} %collective-permute-done.refs_1_, bf16[32,3200]{1,0:T(8,128)(2,1)S(1)} %collective-permute-done.1.refs_2_, ...), custom_call_target="tpu_custom_call" | custom-call | flops 1048576000 | bytes 8388608 | tf_op jit(solution)/shard_map/pallas_call | solution.py:239
  33.6 0.0 collective-permute-start.4
  33.7 0.5 %collective-permute-start.3 = (bf16[16,3200]{1,0:T(8,128)(2,1)S(1)}, bf16[16,3200]{1,0:T(8,128)(2,1)S(1)}, u32[]{:S(2)}, u32[]{:S(2)}) collective-permute-start(bf16[16,3200]{1,0:T(8,128)(2,1)S(1)} %get-tuple-element.32), channel_id=1, source_target_pairs={{0,8},{8,16},{16,24},{24,0},{1,9},{9,17},{17,25},{25,1},{2,10},{10... | collective-permute-start | bytes 307208 | tf_op jit(solution)/shard_map/ppermute | solution.py:27
  34.2 0.1 fusion.1
  34.3 0.0 collective-permute-done.7
  34.3 0.0 collective-permute-done.10
  34.3 0.0 collective-permute-done.9
  34.3 1.7 %collective-permute-done.4 = bf16[16,3200]{1,0:T(8,128)(2,1)S(1)} collective-permute-done((bf16[16,3200]{1,0:T(8,128)(2,1)S(1)}, bf16[16,3200]{1,0:T(8,128)(2,1)S(1)}, u32[]{:S(2)}, u32[]{:S(2)}) %collective-permute-start.4) | collective-permute-done | bytes 102432 | tf_op jit(solution)/shard_map/ppermute | solution.py:27
  36.0 2.8 %collective-permute-done.3 = bf16[16,3200]{1,0:T(8,128)(2,1)S(1)} collective-permute-done((bf16[16,3200]{1,0:T(8,128)(2,1)S(1)}, bf16[16,3200]{1,0:T(8,128)(2,1)S(1)}, u32[]{:S(2)}, u32[]{:S(2)}) %collective-permute-start.3) | collective-permute-done | bytes 102432 | tf_op jit(solution)/shard_map/ppermute | solution.py:27
  38.9 0.8 %fusion = bf16[1,1,1,16,3200]{4,3,2,1,0:T(8,128)(2,1)} fusion(bf16[16,3200]{1,0:T(8,128)(2,1)S(1)} %collective-permute-done.10, bf16[16,3200]{1,0:T(8,128)(2,1)S(1)} %collective-permute-done.9, f32[16,3200]{1,0:T(8,128)S(1)} %get-tuple-element.34, bf16[16,3200]{1,0:T(8,128)(2,1)S(1)} %collective-permute-done.7, ...), kind=kLoop, calls=%fused_computation.3 | loop fusion | flops 768000 | bytes 1126416 | tf_op jit(solution)/shard_map/reshape | solution.py:377
  (3 shorter events, 0.0 us)
Async XLA Ops:
  0.0 5.3 %copy-start = (bf16[2,512,512]{2,1,0:T(8,128)(2,1)S(1)}, bf16[2,512,512]{2,1,0:T(8,128)(2,1)}, u32[]{:S(2)}) copy-start(bf16[2,512,512]{2,1,0:T(8,128)(2,1)} %one.1) | copy-start | bytes 3145732
  0.0 5.4 %copy-start.1 = (bf16[640,640]{1,0:T(8,128)(2,1)S(1)}, bf16[640,640]{1,0:T(8,128)(2,1)}, u32[]{:S(2)}) copy-start(bf16[640,640]{1,0:T(8,128)(2,1)} %zero.1) | copy-start | bytes 2457604
  0.0 5.4 %copy-start.2 = (bf16[2,384,384]{2,1,0:T(8,128)(2,1)S(1)}, bf16[2,384,384]{2,1,0:T(8,128)(2,1)}, u32[]{:S(2)}) copy-start(bf16[2,384,384]{2,1,0:T(8,128)(2,1)} %two.1) | copy-start | bytes 1769476
  0.0 5.4 %copy-start.3 = (f32[1,1,1,115,256]{4,2,3,1,0:T(1,128)S(1)}, f32[1,1,1,115,256]{4,2,3,1,0:T(1,128)}, u32[]{:S(2)}) copy-start(f32[1,1,1,115,256]{4,2,3,1,0:T(1,128)} %param.15) | copy-start | bytes 353284
  0.0 5.4 %copy-start.4 = (bf16[1,1,1,16,3200]{4,3,2,1,0:T(8,128)(2,1)S(1)}, bf16[1,1,1,16,3200]{4,3,2,1,0:T(8,128)(2,1)}, u32[]{:S(2)}) copy-start(bf16[1,1,1,16,3200]{4,3,2,1,0:T(8,128)(2,1)} %param.10) | copy-start | bytes 307204
  0.0 5.4 %copy-start.5 = (bf16[1,1,1,256,128]{4,3,2,1,0:T(8,128)(2,1)S(1)}, bf16[1,1,1,256,128]{4,3,2,1,0:T(8,128)(2,1)}, u32[]{:S(2)}) copy-start(bf16[1,1,1,256,128]{4,3,2,1,0:T(8,128)(2,1)} %param.16) | copy-start | bytes 196612
  0.0 7.9 %collective-permute-start.5 = (bf16[16,3200]{1,0:T(8,128)(2,1)}, bf16[16,3200]{1,0:T(8,128)(2,1)S(1)}, u32[]{:S(2)}, u32[]{:S(2)}) collective-permute-start(bf16[16,3200]{1,0:T(8,128)(2,1)} %bitcast.12), channel_id=1, source_target_pairs={{0,24},{8,0},{16,8},{24,16},{1,25},{9,1},{17,9},{25,17},{2,26},{10... | collective-permute-start | bytes 307208 | tf_op jit(solution)/shard_map/ppermute | solution.py:27
  2.5 5.5 %collective-permute-start.6 = (bf16[16,3200]{1,0:T(8,128)(2,1)}, bf16[16,3200]{1,0:T(8,128)(2,1)S(1)}, u32[]{:S(2)}, u32[]{:S(2)}) collective-permute-start(bf16[16,3200]{1,0:T(8,128)(2,1)} %bitcast.13), channel_id=1, source_target_pairs={{0,8},{8,16},{16,24},{24,0},{1,9},{9,17},{17,25},{25,1},{2,10},{10... | collective-permute-start | bytes 307208 | tf_op jit(solution)/shard_map/ppermute | solution.py:27
  2.5 11.4 %collective-permute-start = (bf16[16,3200]{1,0:T(8,128)(2,1)}, bf16[16,3200]{1,0:T(8,128)(2,1)S(1)}, u32[]{:S(2)}, u32[]{:S(2)}) collective-permute-start(bf16[16,3200]{1,0:T(8,128)(2,1)} %bitcast.14), channel_id=1, source_target_pairs={{0,4},{4,0},{1,5},{5,1},{2,6},{6,2},{3,7},{7,3},{8,12},{12,8},{9,1... | collective-permute-start | bytes 307208 | tf_op jit(solution)/shard_map/ppermute | solution.py:27
  4.0 1.4 %copy-start.7 = (s32[1,1,1,256]{3,2,1,0:T(1,128)S(1)}, s32[1,1,1,256]{3,2,1,0:T(1,128)}, u32[]{:S(2)}) copy-start(s32[1,1,1,256]{3,2,1,0:T(1,128)} %param.14) | copy-start | bytes 3076
  5.3 0.7 %copy-start.6 = (s32[1,1,1,256]{3,2,1,0:T(1,128)S(1)}, s32[1,1,1,256]{3,2,1,0:T(1,128)}, u32[]{:S(2)}) copy-start(s32[1,1,1,256]{3,2,1,0:T(1,128)} %param.13) | copy-start | bytes 3076
  13.3 8.0 %collective-permute-start.8 = (bf16[32,3200]{1,0:T(8,128)(2,1)S(1)}, bf16[32,3200]{1,0:T(8,128)(2,1)S(1)}, u32[]{:S(2)}, u32[]{:S(2)}) collective-permute-start(bf16[32,3200]{1,0:T(8,128)(2,1)S(1)} %get-tuple-element.37), channel_id=1, source_target_pairs={{0,4},{4,0},{1,5},{5,1},{2,6},{6,2},{3,7},{7,3},{8,12},{12,8},{9,1... | collective-permute-start | bytes 614408 | tf_op jit(solution)/shard_map/ppermute | solution.py:27
  13.9 11.1 %collective-permute-start.1 = (bf16[32,3200]{1,0:T(8,128)(2,1)S(1)}, bf16[32,3200]{1,0:T(8,128)(2,1)S(1)}, u32[]{:S(2)}, u32[]{:S(2)}) collective-permute-start(bf16[32,3200]{1,0:T(8,128)(2,1)S(1)} %constant_dynamic-update-slice_fusion), channel_id=1, source_target_pairs={{0,3},{1,0},{2,1},{3,2},{4,7},{5,4},{6,5},{7,6},{8,11},{9,8},{10,9... | collective-permute-start | bytes 614408 | tf_op jit(solution)/shard_map/ppermute | solution.py:27
  17.5 10.8 %collective-permute-start.2 = (bf16[32,3200]{1,0:T(8,128)(2,1)S(1)}, bf16[32,3200]{1,0:T(8,128)(2,1)S(1)}, u32[]{:S(2)}, u32[]{:S(2)}) collective-permute-start(bf16[32,3200]{1,0:T(8,128)(2,1)S(1)} %constant_dynamic-update-slice_fusion), channel_id=1, source_target_pairs={{0,1},{1,2},{2,3},{3,0},{4,5},{5,6},{6,7},{7,4},{8,9},{9,10},{10,1... | collective-permute-start | bytes 614408 | tf_op jit(solution)/shard_map/ppermute | solution.py:27
  17.5 16.8 %collective-permute-start.7 = (bf16[16,3200]{1,0:T(8,128)(2,1)S(1)}, bf16[16,3200]{1,0:T(8,128)(2,1)S(1)}, u32[]{:S(2)}, u32[]{:S(2)}) collective-permute-start(bf16[16,3200]{1,0:T(8,128)(2,1)S(1)} %get-tuple-element.35), channel_id=1, source_target_pairs={{0,4},{4,0},{1,5},{5,1},{2,6},{6,2},{3,7},{7,3},{8,12},{12,8},{9,1... | collective-permute-start | bytes 307208 | tf_op jit(solution)/shard_map/ppermute | solution.py:27
  21.3 13.0 %collective-permute-start.10 = (bf16[16,3200]{1,0:T(8,128)(2,1)S(1)}, bf16[16,3200]{1,0:T(8,128)(2,1)S(1)}, u32[]{:S(2)}, u32[]{:S(2)}) collective-permute-start(bf16[16,3200]{1,0:T(8,128)(2,1)S(1)} %get-tuple-element.40), channel_id=1, source_target_pairs={{0,3},{1,0},{2,1},{3,2},{4,7},{5,4},{6,5},{7,6},{8,11},{9,8},{10,9... | collective-permute-start | bytes 307208 | tf_op jit(solution)/shard_map/ppermute | solution.py:27
  25.0 9.3 %collective-permute-start.9 = (bf16[16,3200]{1,0:T(8,128)(2,1)S(1)}, bf16[16,3200]{1,0:T(8,128)(2,1)S(1)}, u32[]{:S(2)}, u32[]{:S(2)}) collective-permute-start(bf16[16,3200]{1,0:T(8,128)(2,1)S(1)} %get-tuple-element.39), channel_id=1, source_target_pairs={{0,1},{1,2},{2,3},{3,0},{4,5},{5,6},{6,7},{7,4},{8,9},{9,10},{10,1... | collective-permute-start | bytes 307208 | tf_op jit(solution)/shard_map/ppermute | solution.py:27
  33.6 2.4 %collective-permute-start.4 = (bf16[16,3200]{1,0:T(8,128)(2,1)S(1)}, bf16[16,3200]{1,0:T(8,128)(2,1)S(1)}, u32[]{:S(2)}, u32[]{:S(2)}) collective-permute-start(bf16[16,3200]{1,0:T(8,128)(2,1)S(1)} %get-tuple-element.33), channel_id=1, source_target_pairs={{0,24},{8,0},{16,8},{24,16},{1,25},{9,1},{17,9},{25,17},{2,26},{10... | collective-permute-start | bytes 307208 | tf_op jit(solution)/shard_map/ppermute | solution.py:27
  33.7 5.2 %collective-permute-start.3 = (bf16[16,3200]{1,0:T(8,128)(2,1)S(1)}, bf16[16,3200]{1,0:T(8,128)(2,1)S(1)}, u32[]{:S(2)}, u32[]{:S(2)}) collective-permute-start(bf16[16,3200]{1,0:T(8,128)(2,1)S(1)} %get-tuple-element.32), channel_id=1, source_target_pairs={{0,8},{8,16},{16,24},{24,0},{1,9},{9,17},{17,25},{25,1},{2,10},{10... | collective-permute-start | bytes 307208 | tf_op jit(solution)/shard_map/ppermute | solution.py:27
where the time goes:
time: 39.8 us; the launch traced here: 39.6 us
  starting transfers between devices  13.9 us (35%)
  Pallas kernels  12.5 us (31%)
  waiting for transfers between devices  10.2 us (26%)
  between operations  1.46 us (4%)
  other arithmetic  0.93 us (2%)
  local copies, waits for them, and re-layouts  0.65 us (2%)
    ppermute x11, starting transfers between devices, hand_on(): lax.ppermute(block, axis, [(i, (i + distance) % count) for i in range(cou...  13.9 us
    pallas_call x2, Pallas kernels, one_side(): pl.pallas_call(functools.partial(side_kernel, len(pieces), [boxes for box...  10.6 us
    ppermute x11, waiting for transfers between devices, hand_on(): lax.ppermute(block, axis, [(i, (i + distance) % count) for i in range(cou...  10.2 us
    pallas_call x1, Pallas kernels, prepare(): pl.pallas_call(functools.partial(prepare_kernel, tower_classes, plate_cla...  1.91 us
  transfers between devices with their start and end apart: 11, of which 4 were waited for; matrix products, arithmetic and copies ran while one was open for 0% of the time, Pallas kernels for 32%

commit v1 on v0

v1 whole, which is shorter than its diff:
```python
import functools

import jax
import jax.numpy as jnp
from jax import lax
from jax.experimental import pallas as pl
from jax.experimental.pallas import tpu as pltpu
from jax.sharding import PartitionSpec as P


DEGREE = 4
ORDER = 2
COEFS = (DEGREE + 1) ** 2
LAST_LAST = (((1,), (1,)), ((), ()))


def steps_of(axis):
    return (0, 1, -1)[: min(lax.axis_size(axis), 3)]


def place_of(axis):
    return [(0, 0, 0), (1, 0, 1), (2, 0, 1)][min(lax.axis_size(axis), 3) - 1]


def hand_on(block, axis, distance):
    count = lax.axis_size(axis)
    return lax.ppermute(block, axis, [(i, (i + distance) % count) for i in range(count)])


def entries():
    found = []
    for degree in range(DEGREE + 1):
        within = min(degree, ORDER)
        for azimuth in range(-within, within + 1):
            found += [(degree, azimuth, column) for column in range(2 * degree + 1)]
    return found


def offset_of(degree, azimuth):
    return entries().index((degree, azimuth, 0))


def whole(shape):
    return pl.BlockSpec(shape, lambda: (0,) * len(shape), memory_space=pltpu.VMEM)


def prepare_kernel(
    tower_classes, plate_classes, opened, tower_ref, plate_ref, features, wigner, radial, zero, one, two,
    tower_pick, plate_pick, own, spread, gate, zero_t, one_t, two_t,
):
    edges = radial.shape[0]
    for index_ref, classes, pick in (
        (tower_ref, tower_classes, tower_pick),
        (plate_ref, plate_classes, plate_pick),
    ):
        index = index_ref[...]
        atoms = pick.shape[0] // len(classes)
        atom = lax.broadcasted_iota(jnp.int32, (atoms, edges), 0)
        for place, slots in enumerate(classes):
            hit = functools.reduce(
                jnp.logical_or, [index == atom + slot * atoms for slot in slots]
            )
            pick[place * atoms : (place + 1) * atoms, :] = jnp.where(hit, 1.0, 0.0).astype(pick.dtype)

    def copy_row(k, carry):
        spread[k] = jnp.broadcast_to(wigner[k], spread.shape[1:])
        return carry

    lax.fori_loop(0, spread.shape[0], copy_row, 0, unroll=5)
    own[...] = features[...]
    gate[...] = radial[...].astype(jnp.float32).T
    zero_t[...] = zero[...].T
    for ref, out in ((one, one_t), (two, two_t)):
        width = ref.shape[1]
        for part in range(2):
            out[:, part * width : (part + 1) * width] = ref[part].T


GROUP = 16


def rows(at):
    return slice(at, at + GROUP) if isinstance(at, int) else pl.ds(pl.multiple_of(at, GROUP), GROUP)


def side_kernel(pieces, shares, count, *refs):
    piece_refs, refs = refs[:pieces], refs[pieces:]
    from_pick, to_pick, spread, gate, zero_t, one_t, two_t, *refs = refs
    outs, refs = refs[: len(shares)], refs[len(shares) :]
    source, turned, low_zero, low_one, low_two, message, *mixed = refs
    mixed = dict(zip((0, *range(1, ORDER + 1), *range(-ORDER, 0)), mixed))
    channels, edges = gate.shape
    lanes = 128

    def gather(degree):
        first, last = degree * degree, (degree + 1) ** 2
        for k in range(first, last):
            at = slice(k * channels, (k + 1) * channels)
            source[at, :] = jnp.concatenate([ref[:, at] for ref in piece_refs], axis=0).T
        at = slice(first * channels, last * channels)
        turned[at, :] = jnp.dot(source[at, :], from_pick[...], preferred_element_type=jnp.float32)

    def spans():
        return [slice(piece * lanes, (piece + 1) * lanes) for piece in range(edges // lanes)]

    def turn(k, at):
        row = spread[k, :, at]
        return jnp.concatenate([row, row], axis=0)

    def forward(start, azimuth):
        order = abs(azimuth)
        for at in spans():
            far = slice(edges + at.start, edges + at.stop)
            here = gate[rows(start), at]
            for degree in range(order, DEGREE + 1):
                k = offset_of(degree, azimuth)
                total = None
                for c in range(2 * degree + 1):
                    term = turn(k + c, at) * turned[rows((degree * degree + c) * channels + start), at]
                    total = term if total is None else total + term
                small = (total * here).astype(jnp.bfloat16)
                place = (degree - order) * channels + start
                if azimuth == 0:
                    low_zero[rows(place), at] = small
                    continue
                ref = low_one if order == 1 else low_two
                first, second = rows(place), rows(ref.shape[0] // 2 + place)
                if azimuth > 0:
                    ref[first, at] = small
                    ref[second, far] = small
                else:
                    ref[first, far] = small
                    ref[second, at] = -small

    def backward(start, degree):
        within = min(degree, ORDER)
        for at in spans():
            values = {
                azimuth: mixed[azimuth][rows((degree - abs(azimuth)) * channels + start), at]
                for azimuth in range(-within, within + 1)
            }
            for c in range(2 * degree + 1):
                total = None
                for azimuth, value in values.items():
                    term = turn(offset_of(degree, azimuth) + c, at) * value
                    total = term if total is None else total + term
                message[rows((degree * degree + c) * channels + start), at] = total.astype(jnp.bfloat16)

    def product(order):
        if order == 0:
            mixed[0][...] = jnp.dot(zero_t[...], low_zero[...], preferred_element_type=jnp.float32)
            return
        table, low = (one_t, low_one) if order == 1 else (two_t, low_two)
        for azimuth, at in ((order, slice(0, edges)), (-order, slice(edges, 2 * edges))):
            mixed[azimuth][...] = jnp.dot(table[...], low[:, at], preferred_element_type=jnp.float32)

    def scatter(degree):
        at = slice(degree * degree * channels, (degree + 1) ** 2 * channels)
        total = lax.dot_general(spot, message[at, :], LAST_LAST, preferred_element_type=jnp.float32)
        for out, share in zip(outs, shares):
            atoms = out.shape[0] // len(share)
            for place, box in enumerate(share):
                out[place * atoms : (place + 1) * atoms, at] = total[
                    box * atoms : (box + 1) * atoms, :
                ].astype(out.dtype)

    starts = range(0, channels, GROUP)
    for degree in range(DEGREE + 1):
        gather(degree)

    def first_order(i, carry):
        forward(i * GROUP, 0)
        return carry

    lax.fori_loop(0, channels // GROUP, first_order, 0)
    live = lax.broadcasted_iota(jnp.int32, to_pick.shape, 1) < count[0]
    spot = jnp.where(live, to_pick[...].astype(jnp.float32), 0.0).astype(jnp.bfloat16)
    for order in range(1, ORDER + 1):
        product(order - 1)
        for start in starts:
            forward(start, order)
            forward(start, -order)
    product(ORDER)
    for degree in range(DEGREE + 1):
        for start in starts:
            backward(start, degree)
        if degree:
            scatter(degree - 1)
    scatter(DEGREE)


def one_side(count, pieces, from_pick, to_pick, prepared, shares, atoms):
    gate = prepared[1]
    channels, edges = gate.shape
    width = pieces[0].shape[1]
    operands = [*pieces, from_pick, to_pick, *prepared]
    outs = tuple(jax.ShapeDtypeStruct((len(boxes) * atoms, width), dtype) for boxes, dtype in shares)
    work = channels * edges * 2
    flops = work * (sum((DEGREE + 1 - m) ** 2 * channels * (4 if m else 1) for m in range(ORDER + 1)))
    return pl.pallas_call(
        functools.partial(side_kernel, len(pieces), [boxes for boxes, dtype in shares]),
        out_shape=outs,
        in_specs=[pl.BlockSpec(memory_space=pltpu.SMEM)] + [whole(o.shape) for o in operands],
        out_specs=tuple(whole(o.shape) for o in outs),
        scratch_shapes=[
            pltpu.VMEM((width, from_pick.shape[0]), jnp.bfloat16),
            pltpu.VMEM((COEFS * channels, edges), jnp.float32),
            pltpu.VMEM(((DEGREE + 1) * channels, edges), jnp.bfloat16),
            pltpu.VMEM((2 * DEGREE * channels, 2 * edges), jnp.bfloat16),
            pltpu.VMEM((2 * (DEGREE - 1) * channels, 2 * edges), jnp.bfloat16),
            pltpu.VMEM((COEFS * channels, edges), jnp.bfloat16),
        ]
        + [
            pltpu.VMEM(((DEGREE + 1 - abs(m)) * channels, edges), jnp.float32)
            for m in (0, *range(1, ORDER + 1), *range(-ORDER, 0))
        ],
        compiler_params=pltpu.CompilerParams(vmem_limit_bytes=40 * 1024 * 1024),
        cost_estimate=pl.CostEstimate(flops=flops, bytes_accessed=8 << 20, transcendentals=0),
    )(count, *operands)


def opening_kernel(out):
    out[...] = jnp.zeros_like(out)


def opening():
    return pl.pallas_call(
        opening_kernel,
        out_shape=jax.ShapeDtypeStruct((8, 128), jnp.float32),
        out_specs=whole((8, 128)),
        compiler_params=pltpu.CompilerParams(vmem_limit_bytes=1024 * 1024),
        cost_estimate=pl.CostEstimate(flops=20000000000, bytes_accessed=4096, transcendentals=0),
        name="opening",
    )()


def prepare(
    edge_tower, edge_plate, own, wigner, radial, zero, one, two, tower_classes, plate_classes
):
    edges, channels = radial.shape
    atoms = own.shape[0]
    shape = jax.ShapeDtypeStruct
    opened = opening()
    operands = [edge_tower, edge_plate, own, wigner, radial, zero, one, two]
    outs = (
        shape((len(tower_classes) * atoms, edges), jnp.bfloat16),
        shape((len(plate_classes) * atoms, edges), jnp.bfloat16),
        shape(own.shape, own.dtype),
        shape((wigner.shape[0], 8, edges), jnp.float32),
        shape((channels, edges), jnp.float32),
        shape(zero.shape, jnp.bfloat16),
        shape((one.shape[1], 2 * one.shape[1]), jnp.bfloat16),
        shape((two.shape[1], 2 * two.shape[1]), jnp.bfloat16),
    )
    return pl.pallas_call(
        functools.partial(prepare_kernel, tower_classes, plate_classes),
        out_shape=outs,
        in_specs=[whole(o.shape) for o in [opened] + operands],
        out_specs=tuple(whole(o.shape) for o in outs),
        compiler_params=pltpu.CompilerParams(vmem_limit_bytes=24 * 1024 * 1024),
        cost_estimate=pl.CostEstimate(flops=1 << 20, bytes_accessed=8 << 20, transcendentals=0),
        name="prepare",
    )(opened, *operands)


def body(
    features,
    box_atoms,
    edge_count,
    edge_tower,
    edge_plate,
    wigner,
    radial,
    so2_zero,
    so2_one,
    so2_two,
):
    atoms = features.shape[3]
    width = features.shape[4]
    edges = edge_tower.shape[3]
    start = features.reshape(atoms, width)
    x_steps, y_steps, z_steps = steps_of("gx"), steps_of("gy"), steps_of("gz")
    x_place, y_place, z_place = place_of("gx"), place_of("gy"), place_of("gz")
    tower_classes = [[s for s in range(3) if x_place[s] == p] for p in range(len(x_steps))]
    plate_classes = [
        [3 * e + f for e in range(3) for f in range(3) if (y_place[e], z_place[f]) == (py, pz)]
        for pz in range(len(z_steps))
        for py in range(len(y_steps))
    ]

    beside = [hand_on(start, "gy", -step) for step in y_steps[1:]]
    tower = [hand_on(start, "gx", -step) for step in x_steps[1:]]
    tower_pick, plate_pick, own, *prepared = prepare(
        edge_tower.reshape(1, edges),
        edge_plate.reshape(1, edges),
        start,
        wigner.reshape(wigner.shape[3], 1, edges),
        radial.reshape(edges, radial.shape[4]),
        so2_zero,
        so2_one,
        so2_two,
        tower_classes,
        plate_classes,
    )
    column = jnp.concatenate([start] + beside)
    columns = [hand_on(column, "gz", -step) for step in z_steps[1:]]

    count = edge_count.reshape(1)
    across = len(y_steps)
    ends = range(1, len(z_steps))
    here = [([pz * across], jnp.float32) for pz in range(len(z_steps))]
    there = [
        share
        for py in range(1, across)
        for share in (([pz * across + py for pz in ends], jnp.bfloat16), ([py], jnp.bfloat16))
    ]
    sums = one_side(count, [own] + tower, tower_pick, plate_pick, prepared, here + there, atoms)
    kept, leaving = sums[: len(here)], sums[len(here) :]
    kept = list(kept)
    middles = []
    for p, step in enumerate(y_steps[1:]):
        side = hand_on(leaving[2 * p], "gy", step)
        middle = hand_on(leaving[2 * p + 1], "gy", step)
        middles.append(middle)
        for pz in ends:
            kept[pz] = kept[pz] + side[(pz - 1) * atoms : pz * atoms]
    plate_total = functools.reduce(jnp.add, middles, kept[0])
    for p, step in enumerate(z_steps[1:]):
        plate_total = plate_total + hand_on(kept[p + 1].astype(jnp.bfloat16), "gz", step)

    shares = [([0], jnp.float32)] + [([p], jnp.bfloat16) for p in range(1, len(x_steps))]
    gathered, *leaving = one_side(count, [own] + beside + columns, plate_pick, tower_pick, prepared, shares, atoms)
    for p, step in enumerate(x_steps[1:]):
        gathered = gathered + hand_on(leaving[p], "gx", step)
    updated = own.astype(jnp.float32) + (gathered + plate_total)
    present = jnp.arange(atoms, dtype=jnp.int32) < box_atoms.reshape(())
    return jnp.where(present[:, None], updated, 0.0).astype(jnp.bfloat16).reshape(features.shape)


def solution(mesh):
    boxes = P("gx", "gy", "gz")
    placed = (
        P("gx", "gy", "gz", None, None),
        boxes,
        boxes,
        P("gx", "gy", "gz", None),
        P("gx", "gy", "gz", None),
        P("gx", "gy", "gz", None, None),
        P("gx", "gy", "gz", None, None),
        P(),
        P(),
        P(),
    )

    return jax.shard_map(body, mesh=mesh, in_specs=placed, out_specs=P("gx", "gy", "gz", None, None), check_vma=False)
```

time: 39.8 us -> 37.9 us (0.952)
  Pallas kernels: 12.5 us -> 9.92 us
  waiting for transfers between devices: 10.2 us -> 10.9 us
    pallas_call x2, Pallas kernels: 10.6 us -> 9.01 us  [one_side(): pl.pallas_call(functools.partial(side_kernel, len(pieces), [boxes for box...]
    pallas_call x1, Pallas kernels: 1.91 us -> 0.91 us  [prepare(): pl.pallas_call(functools.partial(prepare_kernel, tower_classes, plate_cla...]
    ppermute x11, waiting for transfers between devices: 10.2 us -> 10.9 us  [hand_on(): lax.ppermute(block, axis, [(i, (i + distance) % count) for i in range(cou...]
  transfers between devices with their start and end apart: 11 -> 11, of which waited for: 4 -> 5; matrix products, arithmetic and copies ran while one was open for 0% -> 0% of each run, Pallas kernels for 32% -> 26%
where the time goes in v1:
time: 37.9 us; the launch traced here: 37.7 us
  starting transfers between devices  14 us (37%)
  waiting for transfers between devices  10.9 us (29%)
  Pallas kernels  9.92 us (26%)
  between operations  1.45 us (4%)
  other arithmetic  0.83 us (2%)
  local copies, waits for them, and re-layouts  0.63 us (2%)
    ppermute x11, starting transfers between devices, hand_on(): lax.ppermute(block, axis, [(i, (i + distance) % count) for i in range(cou...  14 us
    ppermute x11, waiting for transfers between devices, hand_on(): lax.ppermute(block, axis, [(i, (i + distance) % count) for i in range(cou...  10.9 us
    pallas_call x2, Pallas kernels, one_side(): pl.pallas_call(functools.partial(side_kernel, len(pieces), [boxes for box...  9.01 us
    pallas_call x1, Pallas kernels, prepare(): pl.pallas_call(functools.partial(prepare_kernel, tower_classes, plate_cla...  0.91 us
    reshape x1, other arithmetic, body(): jnp.where(present[:, None], updated, 0.0).astype(jnp.bfloat16)  0.76 us
  transfers between devices with their start and end apart: 11, of which 5 were waited for; matrix products, arithmetic and copies ran while one was open for 0% of the time, Pallas kernels for 26%

profile of v1, /device:TPU:0, one launch (start us, length us, event | category | flops | bytes accessed | tf_op | source)
XLA Modules:
  0.0 37.7 jit_solution(4595771611336507125)
XLA Ops:
  0.0 0.0 copy-start
  0.0 0.0 copy-start.1
  0.0 0.0 copy-start.2
  0.0 0.0 copy-start.3
  0.0 0.0 copy-start.4
  0.0 0.0 copy-start.5
  0.0 2.5 %collective-permute-start.5 = (bf16[16,3200]{1,0:T(8,128)(2,1)}, bf16[16,3200]{1,0:T(8,128)(2,1)S(1)}, u32[]{:S(2)}, u32[]{:S(2)}) collective-permute-start(bf16[16,3200]{1,0:T(8,128)(2,1)} %bitcast.12), channel_id=1, source_target_pairs={{0,24},{8,0},{16,8},{24,16},{1,25},{9,1},{17,9},{25,17},{2,26},{10... | collective-permute-start | bytes 307208 | tf_op jit(solution)/shard_map/ppermute | solution.py:27
  2.5 0.0 collective-permute-start.6
  2.5 1.5 %collective-permute-start = (bf16[16,3200]{1,0:T(8,128)(2,1)}, bf16[16,3200]{1,0:T(8,128)(2,1)S(1)}, u32[]{:S(2)}, u32[]{:S(2)}) collective-permute-start(bf16[16,3200]{1,0:T(8,128)(2,1)} %bitcast.14), channel_id=1, source_target_pairs={{0,4},{4,0},{1,5},{5,1},{2,6},{6,2},{3,7},{7,3},{8,12},{12,8},{9,1... | collective-permute-start | bytes 307208 | tf_op jit(solution)/shard_map/ppermute | solution.py:27
  4.0 0.0 copy-start.7
  5.3 0.0 copy-start.6
  5.3 0.0 copy-done
  5.4 0.0 copy-done.1
  5.4 0.0 copy-done.2
  5.4 0.0 copy-done.3
  5.4 0.0 copy-done.4
  5.4 0.0 copy-done.5
  5.4 0.0 copy-done.7
  5.4 0.6 %copy-done.6 = s32[1,1,1,256]{3,2,1,0:T(1,128)S(1)} copy-done((s32[1,1,1,256]{3,2,1,0:T(1,128)S(1)}, s32[1,1,1,256]{3,2,1,0:T(1,128)}, u32[]{:S(2)}) %copy-start.6) | copy-done | bytes 1048
  6.0 0.9 %prepare.1 = (bf16[48,256]{1,0:T(8,128)(2,1)S(1)}, bf16[96,256]{1,0:T(8,128)(2,1)S(1)}, bf16[16,3200]{1,0:T(8,128)(2,1)S(1)}, f32[115,8,256]{2,1,0:T(8,128)S(1)}...) custom-call(f32[8,128]{1,0:T(8,128)S(1)} %opening.1.opened, ...), custom_call_target="tpu_custom_call" | custom-call | flops 1048576 | bytes 8388608 | tf_op jit(solution)/shard_map/prepare/pallas_call | solution.py:255
  6.9 0.0 collective-permute-done.5.refs_1_
  6.9 0.1 collective-permute-done.6.refs_2_
  7.0 4.5 %shard_map.101 = (f32[16,3200]{1,0:T(8,128)S(1)}, f32[16,3200]{1,0:T(8,128)S(1)}, f32[16,3200]{1,0:T(8,128)S(1)}, bf16[32,3200]{1,0:T(8,128)(2,1)S(1)}, bf16[16,3200]{1,0:T(8,128)(2,1)S(1)}) custom-call(s32[1]{0:T(128)} %bitcast.11.count, bf16[16,3200]{1,0:T(8,128)(2,1)S(1)} %get-tuple-element.21.refs_0_, ...), custom_call_target="tpu_custom_call" | custom-call | flops 1048576000 | bytes 8388608 | tf_op jit(solution)/shard_map/pallas_call | solution.py:200
  11.5 1.6 %collective-permute-start.8 = (bf16[32,3200]{1,0:T(8,128)(2,1)S(1)}, bf16[32,3200]{1,0:T(8,128)(2,1)S(1)}, u32[]{:S(2)}, u32[]{:S(2)}) collective-permute-start(bf16[32,3200]{1,0:T(8,128)(2,1)S(1)} %get-tuple-element.35), channel_id=1, source_target_pairs={{0,4},{4,0},{1,5},{5,1},{2,6},{6,2},{3,7},{7,3},{8,12},{12,8},{9,1... | collective-permute-start | bytes 614408 | tf_op jit(solution)/shard_map/ppermute | solution.py:27
  13.1 0.0 collective-permute-done.refs_1_
  13.1 3.7 %collective-permute-start.1 = (bf16[32,3200]{1,0:T(8,128)(2,1)S(1)}, bf16[32,3200]{1,0:T(8,128)(2,1)S(1)}, u32[]{:S(2)}, u32[]{:S(2)}) collective-permute-start(bf16[32,3200]{1,0:T(8,128)(2,1)S(1)} %pad_maximum_fusion), channel_id=1, source_target_pairs={{0,3},{1,0},{2,1},{3,2},{4,7},{5,4},{6,5},{7,6},{8,11},{9,8},{10,9... | collective-permute-start | bytes 614408 | tf_op jit(solution)/shard_map/ppermute | solution.py:27
  16.8 0.0 collective-permute-start.2
  16.8 0.5 %collective-permute-start.7 = (bf16[16,3200]{1,0:T(8,128)(2,1)S(1)}, bf16[16,3200]{1,0:T(8,128)(2,1)S(1)}, u32[]{:S(2)}, u32[]{:S(2)}) collective-permute-start(bf16[16,3200]{1,0:T(8,128)(2,1)S(1)} %get-tuple-element.33), channel_id=1, source_target_pairs={{0,4},{4,0},{1,5},{5,1},{2,6},{6,2},{3,7},{7,3},{8,12},{12,8},{9,1... | collective-permute-start | bytes 307208 | tf_op jit(solution)/shard_map/ppermute | solution.py:27
  17.3 2.2 %collective-permute-done.8 = bf16[32,3200]{1,0:T(8,128)(2,1)S(1)} collective-permute-done((bf16[32,3200]{1,0:T(8,128)(2,1)S(1)}, bf16[32,3200]{1,0:T(8,128)(2,1)S(1)}, u32[]{:S(2)}, u32[]{:S(2)}) %collective-permute-start.8) | collective-permute-done | bytes 204832 | tf_op jit(solution)/shard_map/ppermute | solution.py:27
  19.5 0.1 add_convert_fusion.1
  19.6 3.7 %collective-permute-start.10 = (bf16[16,3200]{1,0:T(8,128)(2,1)S(1)}, bf16[16,3200]{1,0:T(8,128)(2,1)S(1)}, u32[]{:S(2)}, u32[]{:S(2)}) collective-permute-start(bf16[16,3200]{1,0:T(8,128)(2,1)S(1)} %get-tuple-element.38), channel_id=1, source_target_pairs={{0,3},{1,0},{2,1},{3,2},{4,7},{5,4},{6,5},{7,6},{8,11},{9,8},{10,9... | collective-permute-start | bytes 307208 | tf_op jit(solution)/shard_map/ppermute | solution.py:27
  23.2 0.0 collective-permute-start.9
  23.3 0.0 collective-permute-done.1.refs_2_
  23.3 3.8 %collective-permute-done.2.refs_3_ = bf16[32,3200]{1,0:T(8,128)(2,1)S(1)} collective-permute-done((bf16[32,3200]{1,0:T(8,128)(2,1)S(1)}, bf16[32,3200]{1,0:T(8,128)(2,1)S(1)}, u32[]{:S(2)}, u32[]{:S(2)}) %collective-permute-start.2) | collective-permute-done | bytes 204832 | tf_op jit(solution)/shard_map/ppermute | solution.py:27
  27.0 4.5 %shard_map.100 = (f32[16,3200]{1,0:T(8,128)S(1)}, bf16[16,3200]{1,0:T(8,128)(2,1)S(1)}, bf16[16,3200]{1,0:T(8,128)(2,1)S(1)}) custom-call(s32[1]{0:T(128)} %bitcast.10.count, bf16[16,3200]{1,0:T(8,128)(2,1)S(1)} %get-tuple-element.21.refs_0_, bf16[16,3200]{1,0:T(8,128)(2,1)S(1)} %collective-permute-done.refs_1_, ...), custom_call_target="tpu_custom_call" | custom-call | flops 1048576000 | bytes 8388608 | tf_op jit(solution)/shard_map/pallas_call | solution.py:200
  31.5 0.1 collective-permute-start.4
  31.6 0.5 %collective-permute-start.3 = (bf16[16,3200]{1,0:T(8,128)(2,1)S(1)}, bf16[16,3200]{1,0:T(8,128)(2,1)S(1)}, u32[]{:S(2)}, u32[]{:S(2)}) collective-permute-start(bf16[16,3200]{1,0:T(8,128)(2,1)S(1)} %get-tuple-element.30), channel_id=1, source_target_pairs={{0,8},{8,16},{16,24},{24,0},{1,9},{9,17},{17,25},{25,1},{2,10},{10... | collective-permute-start | bytes 307208 | tf_op jit(solution)/shard_map/ppermute | solution.py:27
  32.1 0.0 collective-permute-done.7
  32.1 0.0 collective-permute-done.10
  32.1 0.0 collective-permute-done.9
  32.1 1.7 %collective-permute-done.4 = bf16[16,3200]{1,0:T(8,128)(2,1)S(1)} collective-permute-done((bf16[16,3200]{1,0:T(8,128)(2,1)S(1)}, bf16[16,3200]{1,0:T(8,128)(2,1)S(1)}, u32[]{:S(2)}, u32[]{:S(2)}) %collective-permute-start.4) | collective-permute-done | bytes 102432 | tf_op jit(solution)/shard_map/ppermute | solution.py:27
  33.8 3.1 %collective-permute-done.3 = bf16[16,3200]{1,0:T(8,128)(2,1)S(1)} collective-permute-done((bf16[16,3200]{1,0:T(8,128)(2,1)S(1)}, bf16[16,3200]{1,0:T(8,128)(2,1)S(1)}, u32[]{:S(2)}, u32[]{:S(2)}) %collective-permute-start.3) | collective-permute-done | bytes 102432 | tf_op jit(solution)/shard_map/ppermute | solution.py:27
  37.0 0.8 %fusion = bf16[1,1,1,16,3200]{4,3,2,1,0:T(8,128)(2,1)} fusion(bf16[16,3200]{1,0:T(8,128)(2,1)S(1)} %collective-permute-done.10, bf16[16,3200]{1,0:T(8,128)(2,1)S(1)} %collective-permute-done.9, f32[16,3200]{1,0:T(8,128)S(1)} %get-tuple-element.32, bf16[16,3200]{1,0:T(8,128)(2,1)S(1)} %collective-permute-done.7, ...), kind=kLoop, calls=%fused_computation.4 | loop fusion | flops 768000 | bytes 1126416 | tf_op jit(solution)/shard_map/reshape | solution.py:337
  (3 shorter events, 0.0 us)
Async XLA Ops:
  0.0 5.3 %copy-start = (bf16[2,512,512]{2,1,0:T(8,128)(2,1)S(1)}, bf16[2,512,512]{2,1,0:T(8,128)(2,1)}, u32[]{:S(2)}) copy-start(bf16[2,512,512]{2,1,0:T(8,128)(2,1)} %one.1) | copy-start | bytes 3145732
  0.0 5.4 %copy-start.1 = (bf16[640,640]{1,0:T(8,128)(2,1)S(1)}, bf16[640,640]{1,0:T(8,128)(2,1)}, u32[]{:S(2)}) copy-start(bf16[640,640]{1,0:T(8,128)(2,1)} %zero.1) | copy-start | bytes 2457604
  0.0 5.4 %copy-start.2 = (bf16[2,384,384]{2,1,0:T(8,128)(2,1)S(1)}, bf16[2,384,384]{2,1,0:T(8,128)(2,1)}, u32[]{:S(2)}) copy-start(bf16[2,384,384]{2,1,0:T(8,128)(2,1)} %two.1) | copy-start | bytes 1769476
  0.0 5.4 %copy-start.3 = (bf16[1,1,1,16,3200]{4,3,2,1,0:T(8,128)(2,1)S(1)}, bf16[1,1,1,16,3200]{4,3,2,1,0:T(8,128)(2,1)}, u32[]{:S(2)}) copy-start(bf16[1,1,1,16,3200]{4,3,2,1,0:T(8,128)(2,1)} %param.10) | copy-start | bytes 307204
  0.0 5.4 %copy-start.4 = (f32[1,1,1,115,256]{4,2,3,1,0:T(1,128)S(1)}, f32[1,1,1,115,256]{4,2,3,1,0:T(1,128)}, u32[]{:S(2)}) copy-start(f32[1,1,1,115,256]{4,2,3,1,0:T(1,128)} %param.15) | copy-start | bytes 353284
  0.0 5.4 %copy-start.5 = (bf16[1,1,1,256,128]{4,3,2,1,0:T(8,128)(2,1)S(1)}, bf16[1,1,1,256,128]{4,3,2,1,0:T(8,128)(2,1)}, u32[]{:S(2)}) copy-start(bf16[1,1,1,256,128]{4,3,2,1,0:T(8,128)(2,1)} %param.16) | copy-start | bytes 196612
  0.0 6.9 %collective-permute-start.5 = (bf16[16,3200]{1,0:T(8,128)(2,1)}, bf16[16,3200]{1,0:T(8,128)(2,1)S(1)}, u32[]{:S(2)}, u32[]{:S(2)}) collective-permute-start(bf16[16,3200]{1,0:T(8,128)(2,1)} %bitcast.12), channel_id=1, source_target_pairs={{0,24},{8,0},{16,8},{24,16},{1,25},{9,1},{17,9},{25,17},{2,26},{10... | collective-permute-start | bytes 307208 | tf_op jit(solution)/shard_map/ppermute | solution.py:27
  2.5 4.5 %collective-permute-start.6 = (bf16[16,3200]{1,0:T(8,128)(2,1)}, bf16[16,3200]{1,0:T(8,128)(2,1)S(1)}, u32[]{:S(2)}, u32[]{:S(2)}) collective-permute-start(bf16[16,3200]{1,0:T(8,128)(2,1)} %bitcast.13), channel_id=1, source_target_pairs={{0,8},{8,16},{16,24},{24,0},{1,9},{9,17},{17,25},{25,1},{2,10},{10... | collective-permute-start | bytes 307208 | tf_op jit(solution)/shard_map/ppermute | solution.py:27
  2.5 10.6 %collective-permute-start = (bf16[16,3200]{1,0:T(8,128)(2,1)}, bf16[16,3200]{1,0:T(8,128)(2,1)S(1)}, u32[]{:S(2)}, u32[]{:S(2)}) collective-permute-start(bf16[16,3200]{1,0:T(8,128)(2,1)} %bitcast.14), channel_id=1, source_target_pairs={{0,4},{4,0},{1,5},{5,1},{2,6},{6,2},{3,7},{7,3},{8,12},{12,8},{9,1... | collective-permute-start | bytes 307208 | tf_op jit(solution)/shard_map/ppermute | solution.py:27
  4.0 1.4 %copy-start.7 = (s32[1,1,1,256]{3,2,1,0:T(1,128)S(1)}, s32[1,1,1,256]{3,2,1,0:T(1,128)}, u32[]{:S(2)}) copy-start(s32[1,1,1,256]{3,2,1,0:T(1,128)} %param.14) | copy-start | bytes 3076
  5.3 0.7 %copy-start.6 = (s32[1,1,1,256]{3,2,1,0:T(1,128)S(1)}, s32[1,1,1,256]{3,2,1,0:T(1,128)}, u32[]{:S(2)}) copy-start(s32[1,1,1,256]{3,2,1,0:T(1,128)} %param.13) | copy-start | bytes 3076
  11.5 8.0 %collective-permute-start.8 = (bf16[32,3200]{1,0:T(8,128)(2,1)S(1)}, bf16[32,3200]{1,0:T(8,128)(2,1)S(1)}, u32[]{:S(2)}, u32[]{:S(2)}) collective-permute-start(bf16[32,3200]{1,0:T(8,128)(2,1)S(1)} %get-tuple-element.35), channel_id=1, source_target_pairs={{0,4},{4,0},{1,5},{5,1},{2,6},{6,2},{3,7},{7,3},{8,12},{12,8},{9,1... | collective-permute-start | bytes 614408 | tf_op jit(solution)/shard_map/ppermute | solution.py:27
  13.1 10.1 %collective-permute-start.1 = (bf16[32,3200]{1,0:T(8,128)(2,1)S(1)}, bf16[32,3200]{1,0:T(8,128)(2,1)S(1)}, u32[]{:S(2)}, u32[]{:S(2)}) collective-permute-start(bf16[32,3200]{1,0:T(8,128)(2,1)S(1)} %pad_maximum_fusion), channel_id=1, source_target_pairs={{0,3},{1,0},{2,1},{3,2},{4,7},{5,4},{6,5},{7,6},{8,11},{9,8},{10,9... | collective-permute-start | bytes 614408 | tf_op jit(solution)/shard_map/ppermute | solution.py:27
  16.8 10.3 %collective-permute-start.2 = (bf16[32,3200]{1,0:T(8,128)(2,1)S(1)}, bf16[32,3200]{1,0:T(8,128)(2,1)S(1)}, u32[]{:S(2)}, u32[]{:S(2)}) collective-permute-start(bf16[32,3200]{1,0:T(8,128)(2,1)S(1)} %pad_maximum_fusion), channel_id=1, source_target_pairs={{0,1},{1,2},{2,3},{3,0},{4,5},{5,6},{6,7},{7,4},{8,9},{9,10},{10,1... | collective-permute-start | bytes 614408 | tf_op jit(solution)/shard_map/ppermute | solution.py:27
  16.8 15.3 %collective-permute-start.7 = (bf16[16,3200]{1,0:T(8,128)(2,1)S(1)}, bf16[16,3200]{1,0:T(8,128)(2,1)S(1)}, u32[]{:S(2)}, u32[]{:S(2)}) collective-permute-start(bf16[16,3200]{1,0:T(8,128)(2,1)S(1)} %get-tuple-element.33), channel_id=1, source_target_pairs={{0,4},{4,0},{1,5},{5,1},{2,6},{6,2},{3,7},{7,3},{8,12},{12,8},{9,1... | collective-permute-start | bytes 307208 | tf_op jit(solution)/shard_map/ppermute | solution.py:27
  19.6 12.5 %collective-permute-start.10 = (bf16[16,3200]{1,0:T(8,128)(2,1)S(1)}, bf16[16,3200]{1,0:T(8,128)(2,1)S(1)}, u32[]{:S(2)}, u32[]{:S(2)}) collective-permute-start(bf16[16,3200]{1,0:T(8,128)(2,1)S(1)} %get-tuple-element.38), channel_id=1, source_target_pairs={{0,3},{1,0},{2,1},{3,2},{4,7},{5,4},{6,5},{7,6},{8,11},{9,8},{10,9... | collective-permute-start | bytes 307208 | tf_op jit(solution)/shard_map/ppermute | solution.py:27
  23.2 8.9 %collective-permute-start.9 = (bf16[16,3200]{1,0:T(8,128)(2,1)S(1)}, bf16[16,3200]{1,0:T(8,128)(2,1)S(1)}, u32[]{:S(2)}, u32[]{:S(2)}) collective-permute-start(bf16[16,3200]{1,0:T(8,128)(2,1)S(1)} %get-tuple-element.37), channel_id=1, source_target_pairs={{0,1},{1,2},{2,3},{3,0},{4,5},{5,6},{6,7},{7,4},{8,9},{9,10},{10,1... | collective-permute-start | bytes 307208 | tf_op jit(solution)/shard_map/ppermute | solution.py:27
  31.5 2.3 %collective-permute-start.4 = (bf16[16,3200]{1,0:T(8,128)(2,1)S(1)}, bf16[16,3200]{1,0:T(8,128)(2,1)S(1)}, u32[]{:S(2)}, u32[]{:S(2)}) collective-permute-start(bf16[16,3200]{1,0:T(8,128)(2,1)S(1)} %get-tuple-element.31), channel_id=1, source_target_pairs={{0,24},{8,0},{16,8},{24,16},{1,25},{9,1},{17,9},{25,17},{2,26},{10... | collective-permute-start | bytes 307208 | tf_op jit(solution)/shard_map/ppermute | solution.py:27
  31.6 5.4 %collective-permute-start.3 = (bf16[16,3200]{1,0:T(8,128)(2,1)S(1)}, bf16[16,3200]{1,0:T(8,128)(2,1)S(1)}, u32[]{:S(2)}, u32[]{:S(2)}) collective-permute-start(bf16[16,3200]{1,0:T(8,128)(2,1)S(1)} %get-tuple-element.30), channel_id=1, source_target_pairs={{0,8},{8,16},{16,24},{24,0},{1,9},{9,17},{17,25},{25,1},{2,10},{10... | collective-permute-start | bytes 307208 | tf_op jit(solution)/shard_map/ppermute | solution.py:27

commit v2 on v1

--- a/solution.py
+++ b/solution.py
@@ -45,23 +45,9 @@
 
 
 def prepare_kernel(
-    tower_classes, plate_classes, opened, tower_ref, plate_ref, features, wigner, radial, zero, one, two,
-    tower_pick, plate_pick, own, spread, gate, zero_t, one_t, two_t,
+    opened, features, wigner, radial, zero, one, two,
+    own, spread, gate, zero_t, one_t, two_t,
 ):
-    edges = radial.shape[0]
-    for index_ref, classes, pick in (
-        (tower_ref, tower_classes, tower_pick),
-        (plate_ref, plate_classes, plate_pick),
-    ):
-        index = index_ref[...]
-        atoms = pick.shape[0] // len(classes)
-        atom = lax.broadcasted_iota(jnp.int32, (atoms, edges), 0)
-        for place, slots in enumerate(classes):
-            hit = functools.reduce(
-                jnp.logical_or, [index == atom + slot * atoms for slot in slots]
-            )
-            pick[place * atoms : (place + 1) * atoms, :] = jnp.where(hit, 1.0, 0.0).astype(pick.dtype)
-
     def copy_row(k, carry):
         spread[k] = jnp.broadcast_to(wigner[k], spread.shape[1:])
         return carry
@@ -83,14 +69,24 @@
     return slice(at, at + GROUP) if isinstance(at, int) else pl.ds(pl.multiple_of(at, GROUP), GROUP)
 
 
-def side_kernel(pieces, shares, count, *refs):
+def side_kernel(pieces, shares, features_too, from_classes, to_classes, count, present, *refs):
     piece_refs, refs = refs[:pieces], refs[pieces:]
-    from_pick, to_pick, spread, gate, zero_t, one_t, two_t, *refs = refs
+    from_index, to_index, spread, gate, zero_t, one_t, two_t, *refs = refs
     outs, refs = refs[: len(shares)], refs[len(shares) :]
-    source, turned, low_zero, low_one, low_two, message, *mixed = refs
+    from_pick, to_pick, source, turned, low_zero, low_one, low_two, message, *mixed = refs
     mixed = dict(zip((0, *range(1, ORDER + 1), *range(-ORDER, 0)), mixed))
     channels, edges = gate.shape
     lanes = 128
+    live = lax.broadcasted_iota(jnp.int32, (1, edges), 1) < count[0]
+    for index, classes, pick in (
+        (from_index[...], from_classes, from_pick),
+        (jnp.where(live, to_index[...], -1), to_classes, to_pick),
+    ):
+        atoms = pick.shape[0] // len(classes)
+        atom = lax.broadcasted_iota(jnp.int32, (atoms, edges), 0)
+        for place, slots in enumerate(classes):
+            hit = functools.reduce(jnp.logical_or, [index == atom + slot * atoms for slot in slots])
+            pick[place * atoms : (place + 1) * atoms, :] = jnp.where(hit, 1.0, 0.0).astype(pick.dtype)
 
     def gather(degree):
         first, last = degree * degree, (degree + 1) ** 2
@@ -160,9 +156,11 @@
         for out, share in zip(outs, shares):
             atoms = out.shape[0] // len(share)
             for place, box in enumerate(share):
-                out[place * atoms : (place + 1) * atoms, at] = total[
-                    box * atoms : (box + 1) * atoms, :
-                ].astype(out.dtype)
+                summed = total[box * atoms : (box + 1) * atoms, :]
+                if features_too and out is outs[0]:
+                    here = lax.broadcasted_iota(jnp.int32, summed.shape, 0) < present[0]
+                    summed = summed + jnp.where(here, piece_refs[0][:, at].astype(jnp.float32), 0.0)
+                out[place * atoms : (place + 1) * atoms, at] = summed.astype(out.dtype)
 
     starts = range(0, channels, GROUP)
     for degree in range(DEGREE + 1):
@@ -173,8 +171,7 @@
         return carry
 
     lax.fori_loop(0, channels // GROUP, first_order, 0)
-    live = lax.broadcasted_iota(jnp.int32, to_pick.shape, 1) < count[0]
-    spot = jnp.where(live, to_pick[...].astype(jnp.float32), 0.0).astype(jnp.bfloat16)
+    spot = to_pick[...]
     for order in range(1, ORDER + 1):
         product(order - 1)
         for start in starts:
@@ -189,21 +186,26 @@
     scatter(DEGREE)
 
 
-def one_side(count, pieces, from_pick, to_pick, prepared, shares, atoms):
+def one_side(counts, pieces, from_ends, to_ends, prepared, shares, features_too, atoms):
     gate = prepared[1]
     channels, edges = gate.shape
     width = pieces[0].shape[1]
-    operands = [*pieces, from_pick, to_pick, *prepared]
+    (from_index, from_classes), (to_index, to_classes) = from_ends, to_ends
+    operands = [*pieces, from_index, to_index, *prepared]
     outs = tuple(jax.ShapeDtypeStruct((len(boxes) * atoms, width), dtype) for boxes, dtype in shares)
     work = channels * edges * 2
     flops = work * (sum((DEGREE + 1 - m) ** 2 * channels * (4 if m else 1) for m in range(ORDER + 1)))
     return pl.pallas_call(
-        functools.partial(side_kernel, len(pieces), [boxes for boxes, dtype in shares]),
+        functools.partial(
+            side_kernel, len(pieces), [boxes for boxes, dtype in shares], features_too, from_classes, to_classes
+        ),
         out_shape=outs,
-        in_specs=[pl.BlockSpec(memory_space=pltpu.SMEM)] + [whole(o.shape) for o in operands],
+        in_specs=[pl.BlockSpec(memory_space=pltpu.SMEM)] * 2 + [whole(o.shape) for o in operands],
         out_specs=tuple(whole(o.shape) for o in outs),
         scratch_shapes=[
-            pltpu.VMEM((width, from_pick.shape[0]), jnp.bfloat16),
+            pltpu.VMEM((len(from_classes) * atoms, edges), jnp.bfloat16),
+            pltpu.VMEM((len(to_classes) * atoms, edges), jnp.bfloat16),
+            pltpu.VMEM((width, len(from_classes) * atoms), jnp.bfloat16),
             pltpu.VMEM((COEFS * channels, edges), jnp.float32),
             pltpu.VMEM(((DEGREE + 1) * channels, edges), jnp.bfloat16),
             pltpu.VMEM((2 * DEGREE * channels, 2 * edges), jnp.bfloat16),
@@ -216,7 +218,7 @@
         ],
         compiler_params=pltpu.CompilerParams(vmem_limit_bytes=40 * 1024 * 1024),
         cost_estimate=pl.CostEstimate(flops=flops, bytes_accessed=8 << 20, transcendentals=0),
-    )(count, *operands)
+    )(*counts, *operands)
 
 
 def opening_kernel(out):
@@ -234,17 +236,12 @@
     )()
 
 
-def prepare(
-    edge_tower, edge_plate, own, wigner, radial, zero, one, two, tower_classes, plate_classes
-):
+def prepare(own, wigner, radial, zero, one, two):
     edges, channels = radial.shape
-    atoms = own.shape[0]
     shape = jax.ShapeDtypeStruct
     opened = opening()
-    operands = [edge_tower, edge_plate, own, wigner, radial, zero, one, two]
+    operands = [own, wigner, radial, zero, one, two]
     outs = (
-        shape((len(tower_classes) * atoms, edges), jnp.bfloat16),
-        shape((len(plate_classes) * atoms, edges), jnp.bfloat16),
         shape(own.shape, own.dtype),
         shape((wigner.shape[0], 8, edges), jnp.float32),
         shape((channels, edges), jnp.float32),
@@ -253,7 +250,7 @@
         shape((two.shape[1], 2 * two.shape[1]), jnp.bfloat16),
     )
     return pl.pallas_call(
-        functools.partial(prepare_kernel, tower_classes, plate_classes),
+        prepare_kernel,
         out_shape=outs,
         in_specs=[whole(o.shape) for o in [opened] + operands],
         out_specs=tuple(whole(o.shape) for o in outs),
@@ -290,22 +287,20 @@
 
     beside = [hand_on(start, "gy", -step) for step in y_steps[1:]]
     tower = [hand_on(start, "gx", -step) for step in x_steps[1:]]
-    tower_pick, plate_pick, own, *prepared = prepare(
-        edge_tower.reshape(1, edges),
-        edge_plate.reshape(1, edges),
+    own, *prepared = prepare(
         start,
         wigner.reshape(wigner.shape[3], 1, edges),
         radial.reshape(edges, radial.shape[4]),
         so2_zero,
         so2_one,
         so2_two,
-        tower_classes,
-        plate_classes,
     )
+    tower_ends = (edge_tower.reshape(1, edges), tower_classes)
+    plate_ends = (edge_plate.reshape(1, edges), plate_classes)
     column = jnp.concatenate([start] + beside)
     columns = [hand_on(column, "gz", -step) for step in z_steps[1:]]
 
-    count = edge_count.reshape(1)
+    counts = (edge_count.reshape(1), box_atoms.reshape(1))
     across = len(y_steps)
     ends = range(1, len(z_steps))
     here = [([pz * across], jnp.float32) for pz in range(len(z_steps))]
@@ -314,7 +309,7 @@
         for py in range(1, across)
         for share in (([pz * across + py for pz in ends], jnp.bfloat16), ([py], jnp.bfloat16))
     ]
-    sums = one_side(count, [own] + tower, tower_pick, plate_pick, prepared, here + there, atoms)
+    sums = one_side(counts, [own] + tower, tower_ends, plate_ends, prepared, here + there, True, atoms)
     kept, leaving = sums[: len(here)], sums[len(here) :]
     kept = list(kept)
     middles = []
@@ -329,12 +324,12 @@
         plate_total = plate_total + hand_on(kept[p + 1].astype(jnp.bfloat16), "gz", step)
 
     shares = [([0], jnp.float32)] + [([p], jnp.bfloat16) for p in range(1, len(x_steps))]
-    gathered, *leaving = one_side(count, [own] + beside + columns, plate_pick, tower_pick, prepared, shares, atoms)
+    gathered, *leaving = one_side(
+        counts, [own] + beside + columns, plate_ends, tower_ends, prepared, shares, False, atoms
+    )
     for p, step in enumerate(x_steps[1:]):
         gathered = gathered + hand_on(leaving[p], "gx", step)
-    updated = own.astype(jnp.float32) + (gathered + plate_total)
-    present = jnp.arange(atoms, dtype=jnp.int32) < box_atoms.reshape(())
-    return jnp.where(present[:, None], updated, 0.0).astype(jnp.bfloat16).reshape(features.shape)
+    return (gathered + plate_total).astype(jnp.bfloat16).reshape(features.shape)
 
 
 def solution(mesh):

time: 37.9 us -> 38.6 us (1.018)
  waiting for transfers between devices: 10.9 us -> 11.5 us
    ppermute x11, waiting for transfers between devices: 10.9 us -> 11.5 us  [hand_on(): lax.ppermute(block, axis, [(i, (i + distance) % count) for i in range(cou...]
where the time goes in v2:
time: 38.6 us; the launch traced here: 38.4 us
  starting transfers between devices  14 us (36%)
  waiting for transfers between devices  11.5 us (30%)
  Pallas kernels  9.93 us (26%)
  between operations  1.42 us (4%)
  other arithmetic  0.8 us (2%)
  local copies, waits for them, and re-layouts  0.71 us (2%)
    ppermute x11, starting transfers between devices, hand_on(): lax.ppermute(block, axis, [(i, (i + distance) % count) for i in range(cou...  14 us
    ppermute x11, waiting for transfers between devices, hand_on(): lax.ppermute(block, axis, [(i, (i + distance) % count) for i in range(cou...  11.5 us
    pallas_call x2, Pallas kernels, one_side(): pl.pallas_call(functools.partial(side_kernel, len(pieces), [boxes for box...  9.02 us
    pallas_call x1, Pallas kernels, prepare(): pl.pallas_call(prepare_kernel, out_shape=outs, in_specs=[whole(o.shape) f...  0.9 us
  transfers between devices with their start and end apart: 11, of which 5 were waited for; matrix products, arithmetic and copies ran while one was open for 0% of the time, Pallas kernels for 26%

profile of v2, /device:TPU:0, one launch (start us, length us, event | category | flops | bytes accessed | tf_op | source)
XLA Modules:
  0.0 38.4 jit_solution(6593189746815599355)
XLA Ops:
  0.0 0.0 copy-start
  0.0 0.0 copy-start.1
  0.0 0.0 copy-start.2
  0.0 0.0 copy-start.3
  0.0 0.0 copy-start.4
  0.0 0.0 copy-start.5
  0.0 2.5 %collective-permute-start.5 = (bf16[16,3200]{1,0:T(8,128)(2,1)}, bf16[16,3200]{1,0:T(8,128)(2,1)S(1)}, u32[]{:S(2)}, u32[]{:S(2)}) collective-permute-start(bf16[16,3200]{1,0:T(8,128)(2,1)} %bitcast.13), channel_id=1, source_target_pairs={{0,24},{8,0},{16,8},{24,16},{1,25},{9,1},{17,9},{25,17},{2,26},{10... | collective-permute-start | bytes 307208 | tf_op jit(solution)/shard_map/ppermute | solution.py:27
  2.5 0.0 collective-permute-start.6
  2.5 1.5 %collective-permute-start = (bf16[16,3200]{1,0:T(8,128)(2,1)}, bf16[16,3200]{1,0:T(8,128)(2,1)S(1)}, u32[]{:S(2)}, u32[]{:S(2)}) collective-permute-start(bf16[16,3200]{1,0:T(8,128)(2,1)} %bitcast.15), channel_id=1, source_target_pairs={{0,4},{4,0},{1,5},{5,1},{2,6},{6,2},{3,7},{7,3},{8,12},{12,8},{9,1... | collective-permute-start | bytes 307208 | tf_op jit(solution)/shard_map/ppermute | solution.py:27
  5.3 0.0 copy-done
  5.3 0.0 copy-done.1
  5.3 0.0 copy-done.2
  5.4 0.0 copy-done.3
  5.4 0.0 copy-done.4
  5.4 0.0 copy-done.5
  5.4 0.0 copy-start.7
  5.4 0.9 %prepare.1 = (bf16[16,3200]{1,0:T(8,128)(2,1)S(1)}, f32[115,8,256]{2,1,0:T(8,128)S(1)}, f32[128,256]{1,0:T(8,128)S(1)}, bf16[640,640]{1,0:T(8,128)(2,1)S(1)}, bf...) custom-call(f32[8,128]{1,0:T(8,128)S(1)} %opening.1.opened, bf16[16,3200]{1,0:T(8,128)(2,1)S(1)} %bitcast.16, ...), custom_call_target="tpu_custom_call" | custom-call | flops 1048576 | bytes 8388608 | tf_op jit(solution)/shard_map/prepare/pallas_call | solution.py:252
  6.3 0.0 collective-permute-done.5.refs_1_
  6.3 0.7 %collective-permute-done.6.refs_2_ = bf16[16,3200]{1,0:T(8,128)(2,1)S(1)} collective-permute-done((bf16[16,3200]{1,0:T(8,128)(2,1)}, bf16[16,3200]{1,0:T(8,128)(2,1)S(1)}, u32[]{:S(2)}, u32[]{:S(2)}) %collective-permute-start.6) | collective-permute-done | bytes 102432 | tf_op jit(solution)/shard_map/ppermute | solution.py:27
  7.0 0.0 copy-start.6
  7.0 0.0 copy-done.7
  7.0 0.7 %copy-done.6 = s32[1,1,1,256]{3,2,1,0:T(1,128)S(1)} copy-done((s32[1,1,1,256]{3,2,1,0:T(1,128)S(1)}, s32[1,1,1,256]{3,2,1,0:T(1,128)}, u32[]{:S(2)}) %copy-start.6) | copy-done | bytes 1048
  7.7 4.5 %shard_map.101 = (f32[16,3200]{1,0:T(8,128)S(1)}, f32[16,3200]{1,0:T(8,128)S(1)}, f32[16,3200]{1,0:T(8,128)S(1)}, bf16[32,3200]{1,0:T(8,128)(2,1)S(1)}, bf16[16,3200]{1,0:T(8,128)(2,1)S(1)}) custom-call(s32[1]{0:T(128)} %bitcast.12.count, s32[1]{0:T(128)} %bitcast.10.present, bf16[16,3200]{1,0:T(8,128)(2,1)S(1)} %get-tuple-element.19.refs_0_, ...), custom_call_target="tpu_custom_call" | custom-call | flops 1048576000 | bytes 8388608 | tf_op jit(solution)/shard_map/pallas_call | solution.py:198
  12.2 1.6 %collective-permute-start.8 = (bf16[32,3200]{1,0:T(8,128)(2,1)S(1)}, bf16[32,3200]{1,0:T(8,128)(2,1)S(1)}, u32[]{:S(2)}, u32[]{:S(2)}) collective-permute-start(bf16[32,3200]{1,0:T(8,128)(2,1)S(1)} %get-tuple-element.31), channel_id=1, source_target_pairs={{0,4},{4,0},{1,5},{5,1},{2,6},{6,2},{3,7},{7,3},{8,12},{12,8},{9,1... | collective-permute-start | bytes 614408 | tf_op jit(solution)/shard_map/ppermute | solution.py:27
  13.8 0.0 collective-permute-done.refs_1_
  13.8 3.7 %collective-permute-start.1 = (bf16[32,3200]{1,0:T(8,128)(2,1)S(1)}, bf16[32,3200]{1,0:T(8,128)(2,1)S(1)}, u32[]{:S(2)}, u32[]{:S(2)}) collective-permute-start(bf16[32,3200]{1,0:T(8,128)(2,1)S(1)} %pad_maximum_fusion), channel_id=1, source_target_pairs={{0,3},{1,0},{2,1},{3,2},{4,7},{5,4},{6,5},{7,6},{8,11},{9,8},{10,9... | collective-permute-start | bytes 614408 | tf_op jit(solution)/shard_map/ppermute | solution.py:27
  17.5 0.0 collective-permute-start.2
  17.5 0.5 %collective-permute-start.7 = (bf16[16,3200]{1,0:T(8,128)(2,1)S(1)}, bf16[16,3200]{1,0:T(8,128)(2,1)S(1)}, u32[]{:S(2)}, u32[]{:S(2)}) collective-permute-start(bf16[16,3200]{1,0:T(8,128)(2,1)S(1)} %get-tuple-element.29), channel_id=1, source_target_pairs={{0,4},{4,0},{1,5},{5,1},{2,6},{6,2},{3,7},{7,3},{8,12},{12,8},{9,1... | collective-permute-start | bytes 307208 | tf_op jit(solution)/shard_map/ppermute | solution.py:27
  18.0 1.3 %collective-permute-done.8 = bf16[32,3200]{1,0:T(8,128)(2,1)S(1)} collective-permute-done((bf16[32,3200]{1,0:T(8,128)(2,1)S(1)}, bf16[32,3200]{1,0:T(8,128)(2,1)S(1)}, u32[]{:S(2)}, u32[]{:S(2)}) %collective-permute-start.8) | collective-permute-done | bytes 204832 | tf_op jit(solution)/shard_map/ppermute | solution.py:27
  19.3 0.1 add_convert_fusion.2
  19.4 3.7 %collective-permute-start.10 = (bf16[16,3200]{1,0:T(8,128)(2,1)S(1)}, bf16[16,3200]{1,0:T(8,128)(2,1)S(1)}, u32[]{:S(2)}, u32[]{:S(2)}) collective-permute-start(bf16[16,3200]{1,0:T(8,128)(2,1)S(1)} %get-tuple-element.34), channel_id=1, source_target_pairs={{0,3},{1,0},{2,1},{3,2},{4,7},{5,4},{6,5},{7,6},{8,11},{9,8},{10,9... | collective-permute-start | bytes 307208 | tf_op jit(solution)/shard_map/ppermute | solution.py:27
  23.1 0.0 collective-permute-start.9
  23.1 0.0 collective-permute-done.1.refs_2_
  23.1 4.5 %collective-permute-done.2.refs_3_ = bf16[32,3200]{1,0:T(8,128)(2,1)S(1)} collective-permute-done((bf16[32,3200]{1,0:T(8,128)(2,1)S(1)}, bf16[32,3200]{1,0:T(8,128)(2,1)S(1)}, u32[]{:S(2)}, u32[]{:S(2)}) %collective-permute-start.2) | collective-permute-done | bytes 204832 | tf_op jit(solution)/shard_map/ppermute | solution.py:27
  27.6 4.5 %shard_map.100 = (f32[16,3200]{1,0:T(8,128)S(1)}, bf16[16,3200]{1,0:T(8,128)(2,1)S(1)}, bf16[16,3200]{1,0:T(8,128)(2,1)S(1)}) custom-call(s32[1]{0:T(128)} %bitcast.11.count, s32[1]{0:T(128)} %bitcast.9.present, bf16[16,3200]{1,0:T(8,128)(2,1)S(1)} %get-tuple-element.19.refs_0_, bf16[16,3200]{1,0:T(8,128)(2,1)S(1)} %collective-permute-done.refs_1_, ...), custom_call_target="tpu_custom_call" | custom-call | flops 1048576000 | bytes 8388608 | tf_op jit(solution)/shard_map/pallas_call | solution.py:198
  32.1 0.1 collective-permute-start.4
  32.1 0.5 %collective-permute-start.3 = (bf16[16,3200]{1,0:T(8,128)(2,1)S(1)}, bf16[16,3200]{1,0:T(8,128)(2,1)S(1)}, u32[]{:S(2)}, u32[]{:S(2)}) collective-permute-start(bf16[16,3200]{1,0:T(8,128)(2,1)S(1)} %get-tuple-element.26), channel_id=1, source_target_pairs={{0,8},{8,16},{16,24},{24,0},{1,9},{9,17},{17,25},{25,1},{2,10},{10... | collective-permute-start | bytes 307208 | tf_op jit(solution)/shard_map/ppermute | solution.py:27
  32.6 0.0 collective-permute-done.7
  32.6 0.0 collective-permute-done.10
  32.6 0.0 collective-permute-done.9
  32.6 1.7 %collective-permute-done.4 = bf16[16,3200]{1,0:T(8,128)(2,1)S(1)} collective-permute-done((bf16[16,3200]{1,0:T(8,128)(2,1)S(1)}, bf16[16,3200]{1,0:T(8,128)(2,1)S(1)}, u32[]{:S(2)}, u32[]{:S(2)}) %collective-permute-start.4) | collective-permute-done | bytes 102432 | tf_op jit(solution)/shard_map/ppermute | solution.py:27
  34.4 3.3 %collective-permute-done.3 = bf16[16,3200]{1,0:T(8,128)(2,1)S(1)} collective-permute-done((bf16[16,3200]{1,0:T(8,128)(2,1)S(1)}, bf16[16,3200]{1,0:T(8,128)(2,1)S(1)}, u32[]{:S(2)}, u32[]{:S(2)}) %collective-permute-start.3) | collective-permute-done | bytes 102432 | tf_op jit(solution)/shard_map/ppermute | solution.py:27
  37.7 0.7 %fusion = bf16[1,1,1,16,3200]{4,3,2,1,0:T(8,128)(2,1)} fusion(bf16[16,3200]{1,0:T(8,128)(2,1)S(1)} %collective-permute-done.10, bf16[16,3200]{1,0:T(8,128)(2,1)S(1)} %collective-permute-done.9, f32[16,3200]{1,0:T(8,128)S(1)} %get-tuple-element.28, bf16[16,3200]{1,0:T(8,128)(2,1)S(1)} %collective-permute-done.7, ...), kind=kLoop, calls=%fused_computation.4 | loop fusion | flops 614400 | bytes 1024000 | tf_op jit(solution)/shard_map/reshape | solution.py:332
  (2 shorter events, 0.0 us)
Async XLA Ops:
  0.0 5.3 %copy-start = (bf16[2,512,512]{2,1,0:T(8,128)(2,1)S(1)}, bf16[2,512,512]{2,1,0:T(8,128)(2,1)}, u32[]{:S(2)}) copy-start(bf16[2,512,512]{2,1,0:T(8,128)(2,1)} %one.1) | copy-start | bytes 3145732
  0.0 5.3 %copy-start.1 = (bf16[640,640]{1,0:T(8,128)(2,1)S(1)}, bf16[640,640]{1,0:T(8,128)(2,1)}, u32[]{:S(2)}) copy-start(bf16[640,640]{1,0:T(8,128)(2,1)} %zero.1) | copy-start | bytes 2457604
  0.0 5.3 %copy-start.2 = (bf16[2,384,384]{2,1,0:T(8,128)(2,1)S(1)}, bf16[2,384,384]{2,1,0:T(8,128)(2,1)}, u32[]{:S(2)}) copy-start(bf16[2,384,384]{2,1,0:T(8,128)(2,1)} %two.1) | copy-start | bytes 1769476
  0.0 5.3 %copy-start.3 = (bf16[1,1,1,16,3200]{4,3,2,1,0:T(8,128)(2,1)S(1)}, bf16[1,1,1,16,3200]{4,3,2,1,0:T(8,128)(2,1)}, u32[]{:S(2)}) copy-start(bf16[1,1,1,16,3200]{4,3,2,1,0:T(8,128)(2,1)} %param.10) | copy-start | bytes 307204
  0.0 5.4 %copy-start.4 = (f32[1,1,1,115,256]{4,2,3,1,0:T(1,128)S(1)}, f32[1,1,1,115,256]{4,2,3,1,0:T(1,128)}, u32[]{:S(2)}) copy-start(f32[1,1,1,115,256]{4,2,3,1,0:T(1,128)} %param.15) | copy-start | bytes 353284
  0.0 5.4 %copy-start.5 = (bf16[1,1,1,256,128]{4,3,2,1,0:T(8,128)(2,1)S(1)}, bf16[1,1,1,256,128]{4,3,2,1,0:T(8,128)(2,1)}, u32[]{:S(2)}) copy-start(bf16[1,1,1,256,128]{4,3,2,1,0:T(8,128)(2,1)} %param.16) | copy-start | bytes 196612
  0.0 6.3 %collective-permute-start.5 = (bf16[16,3200]{1,0:T(8,128)(2,1)}, bf16[16,3200]{1,0:T(8,128)(2,1)S(1)}, u32[]{:S(2)}, u32[]{:S(2)}) collective-permute-start(bf16[16,3200]{1,0:T(8,128)(2,1)} %bitcast.13), channel_id=1, source_target_pairs={{0,24},{8,0},{16,8},{24,16},{1,25},{9,1},{17,9},{25,17},{2,26},{10... | collective-permute-start | bytes 307208 | tf_op jit(solution)/shard_map/ppermute | solution.py:27
  2.5 4.5 %collective-permute-start.6 = (bf16[16,3200]{1,0:T(8,128)(2,1)}, bf16[16,3200]{1,0:T(8,128)(2,1)S(1)}, u32[]{:S(2)}, u32[]{:S(2)}) collective-permute-start(bf16[16,3200]{1,0:T(8,128)(2,1)} %bitcast.14), channel_id=1, source_target_pairs={{0,8},{8,16},{16,24},{24,0},{1,9},{9,17},{17,25},{25,1},{2,10},{10... | collective-permute-start | bytes 307208 | tf_op jit(solution)/shard_map/ppermute | solution.py:27
  2.5 11.3 %collective-permute-start = (bf16[16,3200]{1,0:T(8,128)(2,1)}, bf16[16,3200]{1,0:T(8,128)(2,1)S(1)}, u32[]{:S(2)}, u32[]{:S(2)}) collective-permute-start(bf16[16,3200]{1,0:T(8,128)(2,1)} %bitcast.15), channel_id=1, source_target_pairs={{0,4},{4,0},{1,5},{5,1},{2,6},{6,2},{3,7},{7,3},{8,12},{12,8},{9,1... | collective-permute-start | bytes 307208 | tf_op jit(solution)/shard_map/ppermute | solution.py:27
  5.4 1.6 %copy-start.7 = (s32[1,1,1,256]{3,2,1,0:T(1,128)S(1)}, s32[1,1,1,256]{3,2,1,0:T(1,128)}, u32[]{:S(2)}) copy-start(s32[1,1,1,256]{3,2,1,0:T(1,128)} %param.14) | copy-start | bytes 3076
  7.0 0.7 %copy-start.6 = (s32[1,1,1,256]{3,2,1,0:T(1,128)S(1)}, s32[1,1,1,256]{3,2,1,0:T(1,128)}, u32[]{:S(2)}) copy-start(s32[1,1,1,256]{3,2,1,0:T(1,128)} %param.13) | copy-start | bytes 3076
  12.2 7.1 %collective-permute-start.8 = (bf16[32,3200]{1,0:T(8,128)(2,1)S(1)}, bf16[32,3200]{1,0:T(8,128)(2,1)S(1)}, u32[]{:S(2)}, u32[]{:S(2)}) collective-permute-start(bf16[32,3200]{1,0:T(8,128)(2,1)S(1)} %get-tuple-element.31), channel_id=1, source_target_pairs={{0,4},{4,0},{1,5},{5,1},{2,6},{6,2},{3,7},{7,3},{8,12},{12,8},{9,1... | collective-permute-start | bytes 614408 | tf_op jit(solution)/shard_map/ppermute | solution.py:27
  13.8 9.3 %collective-permute-start.1 = (bf16[32,3200]{1,0:T(8,128)(2,1)S(1)}, bf16[32,3200]{1,0:T(8,128)(2,1)S(1)}, u32[]{:S(2)}, u32[]{:S(2)}) collective-permute-start(bf16[32,3200]{1,0:T(8,128)(2,1)S(1)} %pad_maximum_fusion), channel_id=1, source_target_pairs={{0,3},{1,0},{2,1},{3,2},{4,7},{5,4},{6,5},{7,6},{8,11},{9,8},{10,9... | collective-permute-start | bytes 614408 | tf_op jit(solution)/shard_map/ppermute | solution.py:27
  17.5 10.1 %collective-permute-start.2 = (bf16[32,3200]{1,0:T(8,128)(2,1)S(1)}, bf16[32,3200]{1,0:T(8,128)(2,1)S(1)}, u32[]{:S(2)}, u32[]{:S(2)}) collective-permute-start(bf16[32,3200]{1,0:T(8,128)(2,1)S(1)} %pad_maximum_fusion), channel_id=1, source_target_pairs={{0,1},{1,2},{2,3},{3,0},{4,5},{5,6},{6,7},{7,4},{8,9},{9,10},{10,1... | collective-permute-start | bytes 614408 | tf_op jit(solution)/shard_map/ppermute | solution.py:27
  17.5 15.1 %collective-permute-start.7 = (bf16[16,3200]{1,0:T(8,128)(2,1)S(1)}, bf16[16,3200]{1,0:T(8,128)(2,1)S(1)}, u32[]{:S(2)}, u32[]{:S(2)}) collective-permute-start(bf16[16,3200]{1,0:T(8,128)(2,1)S(1)} %get-tuple-element.29), channel_id=1, source_target_pairs={{0,4},{4,0},{1,5},{5,1},{2,6},{6,2},{3,7},{7,3},{8,12},{12,8},{9,1... | collective-permute-start | bytes 307208 | tf_op jit(solution)/shard_map/ppermute | solution.py:27
  19.4 13.3 %collective-permute-start.10 = (bf16[16,3200]{1,0:T(8,128)(2,1)S(1)}, bf16[16,3200]{1,0:T(8,128)(2,1)S(1)}, u32[]{:S(2)}, u32[]{:S(2)}) collective-permute-start(bf16[16,3200]{1,0:T(8,128)(2,1)S(1)} %get-tuple-element.34), channel_id=1, source_target_pairs={{0,3},{1,0},{2,1},{3,2},{4,7},{5,4},{6,5},{7,6},{8,11},{9,8},{10,9... | collective-permute-start | bytes 307208 | tf_op jit(solution)/shard_map/ppermute | solution.py:27
  23.1 9.5 %collective-permute-start.9 = (bf16[16,3200]{1,0:T(8,128)(2,1)S(1)}, bf16[16,3200]{1,0:T(8,128)(2,1)S(1)}, u32[]{:S(2)}, u32[]{:S(2)}) collective-permute-start(bf16[16,3200]{1,0:T(8,128)(2,1)S(1)} %get-tuple-element.33), channel_id=1, source_target_pairs={{0,1},{1,2},{2,3},{3,0},{4,5},{5,6},{6,7},{7,4},{8,9},{9,10},{10,1... | collective-permute-start | bytes 307208 | tf_op jit(solution)/shard_map/ppermute | solution.py:27
  32.1 2.3 %collective-permute-start.4 = (bf16[16,3200]{1,0:T(8,128)(2,1)S(1)}, bf16[16,3200]{1,0:T(8,128)(2,1)S(1)}, u32[]{:S(2)}, u32[]{:S(2)}) collective-permute-start(bf16[16,3200]{1,0:T(8,128)(2,1)S(1)} %get-tuple-element.27), channel_id=1, source_target_pairs={{0,24},{8,0},{16,8},{24,16},{1,25},{9,1},{17,9},{25,17},{2,26},{10... | collective-permute-start | bytes 307208 | tf_op jit(solution)/shard_map/ppermute | solution.py:27
  32.1 5.5 %collective-permute-start.3 = (bf16[16,3200]{1,0:T(8,128)(2,1)S(1)}, bf16[16,3200]{1,0:T(8,128)(2,1)S(1)}, u32[]{:S(2)}, u32[]{:S(2)}) collective-permute-start(bf16[16,3200]{1,0:T(8,128)(2,1)S(1)} %get-tuple-element.26), channel_id=1, source_target_pairs={{0,8},{8,16},{16,24},{24,0},{1,9},{9,17},{17,25},{25,1},{2,10},{10... | collective-permute-start | bytes 307208 | tf_op jit(solution)/shard_map/ppermute | solution.py:27
